TPU v7x, 512 devices: a whole 4x8x8 slice. The times are simulated.
512 devices in a mesh: dp: 32 (over x_lo, y, core), head: 16 (over z, x_hi).
Axes of the slice: x: 4 (x_hi: 2, x_lo: 2; x = x_hi * 2 + x_lo), y: 8, z: 8, core: 2. Of those that a mesh axis runs over, the one named last changes fastest.
Arguments:
- hidden_in: bfloat16 [8192, 7168], P('dp', 'head'), may hold values from -6 to 6
- latent_unnormed: bfloat16 [8192, 512], P('dp'), may hold values from -6 to 6
- unrotated_key: bfloat16 [8192, 64], P('dp'), may hold values from -6 to 6
- latent_norm_scale: float32 [512], replicated, may hold values from 0.1 to 1.9
- plain_query_rows: bfloat16 [8192, 16384], P('dp', 'head'), may hold values from -6 to 6
- rotated_query_rows: bfloat16 [8192, 8192], P('dp', 'head'), may hold values from -240 to 240
- key_up_matrix: bfloat16 [512, 16384], P('dp', 'head'), may hold values from -0.25 to 0.25
- value_up_matrix: bfloat16 [512, 16384], P('dp', 'head'), may hold values from -0.25 to 0.25
- output_cotangent: bfloat16 [8192, 16384], P('dp', 'head'), may hold values from -6 to 6
- down_weight: float32 [576, 7168], P('dp', 'head'), may hold values from -0.0625 to 0.0625
- first_moment: float32 [576, 7168], P('dp', 'head'), may hold values from -0.078125 to 0.078125
- second_moment: float32 [576, 7168], P('dp', 'head'), may hold values from 4e-08 to 4e-07
Outputs:
- query_grad_nope: bfloat16 [8192, 16384], P('dp', 'head')
- query_grad_rope: bfloat16 [8192, 8192], P('dp', 'head')
- new_weight: float32 [576, 7168], P('dp', 'head')
- new_first: float32 [576, 7168], P('dp', 'head')
- new_second: float32 [576, 7168], P('dp', 'head')
All inputs are finite; a program needn't handle non-finite values.
Results may differ from a plain program's by a relative error of at most 0.011.
The roundings to bfloat16 on the way count: a program that leaves them out, or rounds other values in their place, can miss the bound.
Values may be sent and summed in bfloat16 or wider, within the bound.
A program may use at most 64 MiB of HBM per device.

v0:
```python
import math

import jax
import jax.numpy as jnp
from jax import lax
from jax.sharding import PartitionSpec as P

SEQUENCE_LENGTH = 256


norm_eps = 1e-06
beta_one = 0.9
beta_two = 0.999
adam_eps = 1e-08
learn_rate = 0.01
decay_rate = 0.1
bias_one = 1.0 - 0.9**2
bias_two = 1.0 - 0.999**2


def angle_tables(positions, rope_width):
    half_width = rope_width // 2
    inverse_freq = jnp.exp(
        jnp.arange(half_width, dtype=jnp.float32) * (-2.0 * math.log(10000.0) / rope_width)
    )
    angles = positions.astype(jnp.float32)[:, None] * inverse_freq[None, :]
    return (jnp.cos(angles), jnp.sin(angles))


def latent_back(
    latent_sum, rope_sum, latent_in, inverse_rms, latent_norm_scale, cos_table, sin_table
):
    latent_width = latent_in.shape[1]
    scaled_grad = latent_norm_scale * latent_sum
    inner_sum = jnp.sum(latent_in * scaled_grad, axis=1, keepdims=True)
    latent_grad = (
        inverse_rms * scaled_grad
        - latent_in * (inverse_rms * inverse_rms * inverse_rms) * inner_sum / latent_width
    )
    half_width = rope_sum.shape[1] // 2
    grad_first = rope_sum[:, :half_width]
    grad_second = rope_sum[:, half_width:]
    rope_grad = jnp.concatenate(
        (
            grad_first * cos_table + grad_second * sin_table,
            grad_second * cos_table - grad_first * sin_table,
        ),
        axis=1,
    )
    return jnp.concatenate((latent_grad, rope_grad), axis=1).astype(jnp.bfloat16)


def local(
    hidden_in,
    latent_unnormed,
    unrotated_key,
    latent_norm_scale,
    plain_query_rows,
    rotated_query_rows,
    key_up_matrix,
    value_up_matrix,
    output_cotangent,
    down_weight,
    first_moment,
    second_moment,
):
    row_count = latent_unnormed.shape[0]
    rope_width = unrotated_key.shape[1]
    head_count = rotated_query_rows.shape[1] // rope_width
    nope_width = plain_query_rows.shape[1] // head_count
    value_width = output_cotangent.shape[1] // head_count
    seq_count = row_count // SEQUENCE_LENGTH
    scale_factor = 1.0 / math.sqrt(nope_width + rope_width)
    positions = jnp.arange(row_count, dtype=jnp.int32) % SEQUENCE_LENGTH
    cos_table, sin_table = angle_tables(positions, rope_width)
    raw_key = unrotated_key.astype(jnp.float32)
    half_width = rope_width // 2
    first_half = raw_key[:, :half_width]
    second_half = raw_key[:, half_width:]
    key_rot = jnp.concatenate(
        (
            first_half * cos_table - second_half * sin_table,
            first_half * sin_table + second_half * cos_table,
        ),
        axis=1,
    ).astype(jnp.bfloat16)
    latent_in = latent_unnormed.astype(jnp.float32)
    inverse_rms = lax.rsqrt(jnp.mean(latent_in * latent_in, axis=1, keepdims=True) + norm_eps)
    latent = (latent_in * inverse_rms * latent_norm_scale).astype(jnp.bfloat16)
    joined = jnp.concatenate((key_up_matrix, value_up_matrix), axis=1)
    split_at = head_count * nope_width
    full_rows = lax.all_gather(joined, "dp", axis=0, tiled=True)
    projected = jnp.dot(latent, full_rows, preferred_element_type=jnp.float32)
    key_nope = (
        projected[:, :split_at]
        .astype(jnp.bfloat16)
        .reshape(seq_count, SEQUENCE_LENGTH, head_count, nope_width)
    )
    value_rows = (
        projected[:, split_at:]
        .astype(jnp.bfloat16)
        .reshape(seq_count, SEQUENCE_LENGTH, head_count, value_width)
    )
    nope_query = plain_query_rows.reshape(seq_count, SEQUENCE_LENGTH, head_count, nope_width)
    rope_query = rotated_query_rows.reshape(seq_count, SEQUENCE_LENGTH, head_count, rope_width)
    grad_rows = output_cotangent.reshape(seq_count, SEQUENCE_LENGTH, head_count, value_width)
    rot_rows = key_rot.reshape(seq_count, SEQUENCE_LENGTH, rope_width)
    scores = (
        jnp.einsum("bthd,bshd->bhts", nope_query, key_nope, preferred_element_type=jnp.float32)
        + jnp.einsum("bthd,bsd->bhts", rope_query, rot_rows, preferred_element_type=jnp.float32)
    ) * scale_factor
    causal = jnp.arange(SEQUENCE_LENGTH)[:, None] >= jnp.arange(SEQUENCE_LENGTH)[None, :]
    scores = jnp.where(causal, scores, -1e30)
    maxima = jnp.max(scores, axis=-1, keepdims=True)
    exponent = jnp.exp(scores - maxima)
    probabilities = exponent / jnp.sum(exponent, axis=-1, keepdims=True)
    prob_low = probabilities.astype(jnp.bfloat16)
    attended = jnp.einsum(
        "bhts,bshd->bthd", prob_low, value_rows, preferred_element_type=jnp.float32
    )
    delta_sum = jnp.einsum("bthd,bthd->bht", grad_rows.astype(jnp.float32), attended)
    grad_probs = jnp.einsum(
        "bthd,bshd->bhts", grad_rows, value_rows, preferred_element_type=jnp.float32
    )
    grad_scores = probabilities * (grad_probs - delta_sum[..., None]) * scale_factor
    score_low = grad_scores.astype(jnp.bfloat16)
    grad_nope_q = jnp.einsum(
        "bhts,bshd->bthd", score_low, key_nope, preferred_element_type=jnp.float32
    ).astype(jnp.bfloat16)
    grad_rope_q = jnp.einsum(
        "bhts,bsd->bthd", score_low, rot_rows, preferred_element_type=jnp.float32
    ).astype(jnp.bfloat16)
    grad_key = jnp.einsum(
        "bhts,bthd->bshd", score_low, nope_query, preferred_element_type=jnp.float32
    ).astype(jnp.bfloat16)
    grad_value = jnp.einsum(
        "bhts,bthd->bshd", prob_low, grad_rows, preferred_element_type=jnp.float32
    ).astype(jnp.bfloat16)
    rope_part = jnp.einsum(
        "bhts,bthd->bsd", score_low, rope_query, preferred_element_type=jnp.float32
    ).reshape(row_count, rope_width)
    grads_joined = jnp.concatenate(
        (
            grad_key.reshape(row_count, split_at),
            grad_value.reshape(row_count, head_count * value_width),
        ),
        axis=1,
    )
    latent_part = jnp.einsum(
        "tk,ck->tc", grads_joined, full_rows, preferred_element_type=jnp.float32
    )
    latent_sum, rope_sum = lax.psum((latent_part, rope_part), "head")
    kv_grad = latent_back(
        latent_sum, rope_sum, latent_in, inverse_rms, latent_norm_scale, cos_table, sin_table
    )
    weight_sum = lax.psum_scatter(
        jnp.einsum("tc,td->cd", kv_grad, hidden_in, preferred_element_type=jnp.float32),
        "dp",
        scatter_dimension=0,
        tiled=True,
    )
    weight_grad = weight_sum / (row_count * lax.axis_size("dp"))
    new_first = beta_one * first_moment + (1.0 - beta_one) * weight_grad
    new_second = beta_two * second_moment + (1.0 - beta_two) * weight_grad * weight_grad
    direction = new_first / bias_one / (jnp.sqrt(new_second / bias_two) + adam_eps)
    new_weight = down_weight - learn_rate * (direction + decay_rate * down_weight)
    return (
        grad_nope_q.reshape(row_count, split_at),
        grad_rope_q.reshape(row_count, head_count * rope_width),
        new_weight,
        new_first,
        new_second,
    )


def solution(mesh):
    placed = (
        P("dp", "head"),
        P("dp", None),
        P("dp", None),
        P(),
        P("dp", "head"),
        P("dp", "head"),
        P("dp", "head"),
        P("dp", "head"),
        P("dp", "head"),
        P("dp", "head"),
        P("dp", "head"),
        P("dp", "head"),
    )
    return jax.shard_map(
        local,
        mesh=mesh,
        in_specs=placed,
        out_specs=(
            P("dp", "head"),
            P("dp", "head"),
            P("dp", "head"),
            P("dp", "head"),
            P("dp", "head"),
        ),
        check_vma=False,
    )
```

profile of v0, /device:TPU:1, one launch (start us, length us, event | category | flops | bytes accessed | tf_op | source)
XLA Modules:
  0.0 376.5 jit_solution(13306628696366333491)
XLA Ops:
  7.2 1.5 pad_maximum_fusion
  8.8 1.2 copy.89
  10.1 0.8 convert_element_type.88
  10.9 1.8 copy.58
  12.8 1.2 copy.69
  14.1 0.6 multiply_multiply_fusion
  14.9 68.9 %all-gather.2.cloned.1.call-done = bf16[512,2048]{1,0:T(8,128)(2,1)} async-done(((bf16[16,2048]{1,0:T(8,128)(2,1)}), bf16[512,2048]{1,0:T(8,128)(2,1)}) %all-gather.2.cloned.1.call-update) | async-done | bytes 2097168 | tf_op jit(solution)/shard_map/all_gather | solution.py:92
  83.8 2.4 convolution_convert_fusion
  86.2 0.9 fusion.53
  87.0 0.2 copy.88
  87.3 0.5 fusion.55
  87.8 0.6 copy-done.8
  88.4 0.6 fusion.54
  89.0 0.3 fusion.6
  89.3 0.3 fusion.14
  89.6 2.1 copy.90
  91.7 2.3 convolution_bitcast_fusion
  94.0 2.6 copy.81
  96.6 1.7 multiply_reduce_fusion
  98.3 0.7 copy.82
  99.0 1.6 convolution_convert_fusion.1
  100.6 0.7 fusion.7
  101.3 0.3 copy-done.5
  101.6 0.5 convolution_convert_fusion.2
  102.1 0.5 copy-done.9
  102.6 1.1 convolution_bitcast_fusion.1
  103.7 1.6 fusion.8
  105.3 1.3 dynamic-slice.4
  107.2 152.2 %all-reduce.5.cloned.1.call-done = (f32[256,64]{0,1:T(8,128)}, f32[256,512]{1,0:T(8,128)}) async-done(((f32[256,64]{0,1:T(8,128)}, f32[256,512]{1,0:T(8,128)}), (f32[256,64]{0,1:T(8,128)}, f32[256,512]{1,0:T(8,128)})) %all-reduce.5.cloned.1.call-update) | async-done | bytes 589840 | tf_op jit(solution)/shard_map/psum | solution.py:152
  259.4 1.2 fusion.22
  260.6 1.0 fusion.45
  261.9 1.3 fusion.21
  263.2 0.4 fusion.23
  263.6 71.5 %fusion = f32[24,448]{1,0:T(8,128)S(1)} fusion(f32[576,448]{1,0:T(8,128)S(1)} %fusion.23), kind=kCustom, calls=%all-reduce-scatter | all-reduce-scatter fusion | flops 344065 | bytes 1077248
  335.1 3.5 collective-permute-start
  338.5 1.3 collective-permute-start.1
  339.8 1.3 collective-permute-start.7
  341.1 0.3 convolution_convert_fusion.3
  341.5 9.0 %collective-permute-start.2 = (f32[24,448]{1,0:T(8,128)S(1)}, f32[24,448]{1,0:T(8,128)S(1)}, u32[]{:S(2)}, u32[]{:S(2)}) collective-permute-start(f32[24,448]{1,0:T(8,128)S(1)} %fusion), channel_id=1, source_target_pairs={{0,48},{16,64},{32,80},{48,96},{64,112},{80,128},{96,144},{112,160... | collective-permute-start | bytes 129032
  350.5 5.4 %collective-permute-start.3 = (f32[24,448]{1,0:T(8,128)S(1)}, f32[24,448]{1,0:T(8,128)S(1)}, u32[]{:S(2)}, u32[]{:S(2)}) collective-permute-start(f32[24,448]{1,0:T(8,128)S(1)} %fusion), channel_id=1, source_target_pairs={{0,64},{16,80},{32,96},{48,112},{64,128},{80,144},{96,160},{112,17... | collective-permute-start | bytes 129032
  356.0 2.7 collective-permute-start.4
  358.7 1.6 collective-permute-start.5
  360.3 5.3 %collective-permute-start.6 = (f32[24,448]{1,0:T(8,128)S(1)}, f32[24,448]{1,0:T(8,128)S(1)}, u32[]{:S(2)}, u32[]{:S(2)}) collective-permute-start(f32[24,448]{1,0:T(8,128)S(1)} %fusion), channel_id=1, source_target_pairs={{0,112},{16,128},{32,144},{48,160},{64,176},{80,192},{96,208},{112... | collective-permute-start | bytes 129032
  365.6 0.3 convolution_convert_fusion.4
  365.9 1.0 copy.73
  366.9 0.8 copy.74
  367.8 1.1 concatenate.21
  369.0 0.7 multiply_subtract_fusion
  (72 shorter events, 1.0 us)
Async XLA Ops:
  7.2 256.0 %copy-start = (bf16[256,448]{0,1:T(8,128)(2,1)S(1)}, bf16[256,448]{0,1:T(8,128)(2,1)}, u32[]{:S(2)}) copy-start(bf16[256,448]{0,1:T(8,128)(2,1)} %param.12) | copy-start | bytes 688132
  7.2 5.5 %copy-start.13 = (bf16[256,1024]{1,0:T(8,128)(2,1)S(1)}, bf16[256,1024]{1,0:T(8,128)(2,1)}, u32[]{:S(2)}) copy-start(bf16[256,1024]{1,0:T(8,128)(2,1)} %param.20) | copy-start | bytes 1572868
  7.2 6.8 %copy-start.6 = (bf16[256,512]{1,0:T(8,128)(2,1)S(1)}, bf16[256,512]{1,0:T(8,128)(2,1)}, u32[]{:S(2)}) copy-start(bf16[256,512]{1,0:T(8,128)(2,1)} %param.13) | copy-start | bytes 786436
  7.2 76.6 %all-gather.2.cloned.1.call-start = ((), (), s32[]{:S(2)}) async-start(), calls=%async_computation | async-start | bytes 2162688 | tf_op jit(solution)/shard_map/all_gather | solution.py:92
  8.8 75.0 %copy-start.17 = (f32[512]{0:T(512)S(1)}, f32[512]{0:T(512)}, u32[]{:S(2)}) copy-start(f32[512]{0:T(512)} %param.15) | copy-start | bytes 6148
  8.8 250.6 %all-reduce.5.cloned.1.call-start = ((), (), s32[]{:S(2)}) async-start(), calls=%async_computation.1 | async-start | bytes 1179648 | tf_op jit(solution)/shard_map/psum | solution.py:152
  10.1 77.2 %copy-start.4 = (bf16[256,1024]{0,1:T(8,128)(2,1)}, bf16[256,1024]{0,1:T(8,128)(2,1)S(1)}, u32[]{:S(2)}) copy-start(bf16[256,1024]{0,1:T(8,128)(2,1)S(1)} %copy.89) | copy-start | bytes 1572868
  12.8 73.4 %copy-start.1 = (bf16[32,8,8,128]{3,2,1,0:T(8,128)(2,1)}, bf16[32,8,8,128]{3,2,1,0:T(8,128)(2,1)S(1)}, u32[]{:S(2)}) copy-start(bf16[32,8,8,128]{3,2,1,0:T(8,128)(2,1)S(1)} %copy.91) | copy-start | bytes 1572868
  13.9 73.1 %copy-start.25 = (f32[32]{0:T(128)}, f32[32]{0:T(128)S(1)}, u32[]{:S(2)}) copy-start(f32[32]{0:T(128)S(1)} %multiply_exponential_fusion) | copy-start | bytes 388
  13.9 73.1 %copy-start.22 = (f32[256]{0:T(256)}, f32[256]{0:T(256)S(1)}, u32[]{:S(2)}) copy-start(f32[256]{0:T(256)S(1)} %fusion.48) | copy-start | bytes 3076
  14.7 72.3 %copy-start.19 = (f32[256]{0:T(256)}, f32[256]{0:T(256)S(1)}, u32[]{:S(2)}) copy-start(f32[256]{0:T(256)S(1)} %get-tuple-element.32) | copy-start | bytes 3076
  87.3 1.7 copy-start.2
  87.3 1.1 copy-start.8
  98.9 1.6 copy-start.10
  99.0 1.6 copy-start.12
  99.0 1.6 copy-start.21
  100.6 1.0 copy-start.5
  101.6 0.9 copy-start.9
  101.6 2.0 copy-start.11
  103.7 155.7 %copy-start.7 = (bf16[256,512]{1,0:T(8,128)(2,1)S(1)}, bf16[256,512]{1,0:T(8,128)(2,1)}, u32[]{:S(2)}) copy-start(bf16[256,512]{1,0:T(8,128)(2,1)} %param.13) | copy-start | bytes 786436
  103.7 155.7 %copy-start.18 = (f32[512]{0:T(512)S(1)}, f32[512]{0:T(512)}, u32[]{:S(2)}) copy-start(f32[512]{0:T(512)} %param.15) | copy-start | bytes 6148
  103.7 156.9 %copy-start.23 = (f32[256]{0:T(256)S(1)}, f32[256]{0:T(256)}, u32[]{:S(2)}) copy-start(f32[256]{0:T(256)} %copy-done.22) | copy-start | bytes 3076
  103.7 156.9 %copy-start.26 = (f32[32]{0:T(128)S(1)}, f32[32]{0:T(128)}, u32[]{:S(2)}) copy-start(f32[32]{0:T(128)} %copy-done.25) | copy-start | bytes 388
  103.7 158.2 %copy-start.20 = (f32[256]{0:T(256)S(1)}, f32[256]{0:T(256)}, u32[]{:S(2)}) copy-start(f32[256]{0:T(256)} %copy-done.19) | copy-start | bytes 3076
  103.7 158.2 %copy-start.24 = (f32[256]{0:T(256)S(1)}, f32[256]{0:T(256)}, u32[]{:S(2)}) copy-start(f32[256]{0:T(256)} %get-tuple-element.31) | copy-start | bytes 3076
  261.8 79.3 %copy-start.3 = (bf16[256,1024]{0,1:T(8,128)(2,1)S(1)}, bf16[256,1024]{0,1:T(8,128)(2,1)}, u32[]{:S(2)}) copy-start(bf16[256,1024]{0,1:T(8,128)(2,1)} %copy-done.2) | copy-start | bytes 1572868
  335.1 23.6 %collective-permute-start = (f32[24,448]{1,0:T(8,128)S(1)}, f32[24,448]{1,0:T(8,128)S(1)}, u32[]{:S(2)}, u32[]{:S(2)}) collective-permute-start(f32[24,448]{1,0:T(8,128)S(1)} %fusion), channel_id=1, source_target_pairs={{0,16},{16,32},{32,48},{48,64},{64,80},{80,96},{96,112},{112,128},... | collective-permute-start | bytes 129032
  338.5 21.8 %collective-permute-start.1 = (f32[24,448]{1,0:T(8,128)S(1)}, f32[24,448]{1,0:T(8,128)S(1)}, u32[]{:S(2)}, u32[]{:S(2)}) collective-permute-start(f32[24,448]{1,0:T(8,128)S(1)} %fusion), channel_id=1, source_target_pairs={{0,32},{16,48},{32,64},{48,80},{64,96},{80,112},{96,128},{112,144}... | collective-permute-start | bytes 129032
  339.8 16.1 %collective-permute-start.7 = (f32[18,448]{1,0:T(8,128)S(1)}, f32[18,448]{1,0:T(8,128)S(1)}, u32[]{:S(2)}, u32[]{:S(2)}) collective-permute-start(f32[18,448]{1,0:T(8,128)S(1)} %slice.32), channel_id=1, source_target_pairs={{0,128},{16,144},{32,160},{48,176},{64,192},{80,208},{96,224},{112... | collective-permute-start | bytes 96776
  341.5 27.5 %copy-start.14 = (f32[18,448]{1,0:T(8,128)S(1)}, f32[18,448]{1,0:T(8,128)}, u32[]{:S(2)}) copy-start(f32[18,448]{1,0:T(8,128)} %param.21) | copy-start | bytes 96772
  341.5 27.5 %copy-start.15 = (f32[18,448]{1,0:T(8,128)S(1)}, f32[18,448]{1,0:T(8,128)}, u32[]{:S(2)}) copy-start(f32[18,448]{1,0:T(8,128)} %param.22) | copy-start | bytes 96772
  341.5 27.5 %copy-start.16 = (f32[18,448]{1,0:T(8,128)S(1)}, f32[18,448]{1,0:T(8,128)}, u32[]{:S(2)}) copy-start(f32[18,448]{1,0:T(8,128)} %param.23) | copy-start | bytes 96772
  341.5 26.3 %collective-permute-start.2 = (f32[24,448]{1,0:T(8,128)S(1)}, f32[24,448]{1,0:T(8,128)S(1)}, u32[]{:S(2)}, u32[]{:S(2)}) collective-permute-start(f32[24,448]{1,0:T(8,128)S(1)} %fusion), channel_id=1, source_target_pairs={{0,48},{16,64},{32,80},{48,96},{64,112},{80,128},{96,144},{112,160... | collective-permute-start | bytes 129032
  350.5 17.3 %collective-permute-start.3 = (f32[24,448]{1,0:T(8,128)S(1)}, f32[24,448]{1,0:T(8,128)S(1)}, u32[]{:S(2)}, u32[]{:S(2)}) collective-permute-start(f32[24,448]{1,0:T(8,128)S(1)} %fusion), channel_id=1, source_target_pairs={{0,64},{16,80},{32,96},{48,112},{64,128},{80,144},{96,160},{112,17... | collective-permute-start | bytes 129032
  356.0 11.8 %collective-permute-start.4 = (f32[24,448]{1,0:T(8,128)S(1)}, f32[24,448]{1,0:T(8,128)S(1)}, u32[]{:S(2)}, u32[]{:S(2)}) collective-permute-start(f32[24,448]{1,0:T(8,128)S(1)} %fusion), channel_id=1, source_target_pairs={{0,80},{16,96},{32,112},{48,128},{64,144},{80,160},{96,176},{112,1... | collective-permute-start | bytes 129032
  358.7 9.1 %collective-permute-start.5 = (f32[24,448]{1,0:T(8,128)S(1)}, f32[24,448]{1,0:T(8,128)S(1)}, u32[]{:S(2)}, u32[]{:S(2)}) collective-permute-start(f32[24,448]{1,0:T(8,128)S(1)} %fusion), channel_id=1, source_target_pairs={{0,96},{16,112},{32,128},{48,144},{64,160},{80,176},{96,192},{112,... | collective-permute-start | bytes 129032
  360.3 7.5 %collective-permute-start.6 = (f32[24,448]{1,0:T(8,128)S(1)}, f32[24,448]{1,0:T(8,128)S(1)}, u32[]{:S(2)}, u32[]{:S(2)}) collective-permute-start(f32[24,448]{1,0:T(8,128)S(1)} %fusion), channel_id=1, source_target_pairs={{0,112},{16,128},{32,144},{48,160},{64,176},{80,192},{96,208},{112... | collective-permute-start | bytes 129032
Sparse Core Ops, SparseCore 0:
  10.8 72.9 all-gather.1
  105.4 153.9 all-reduce.4
where the time goes:
time: 379 us; the launch traced here: 377 us
  waiting for transfers between devices  221 us (58%)
  blocking collectives  71.5 us (19%)
  starting transfers between devices  30.2 us (8%)
  local copies, waits for them, and re-layouts  16.7 us (4%)
  between operations  15.2 us (4%)
  matrix products  12.2 us (3%)
  other arithmetic  9.68 us (3%)
    psum x1, waiting for transfers between devices, local(): latent_sum, rope_sum = lax.psum((latent_part, rope_part), 'head')  152 us
    unnamed x1, blocking collectives  71.5 us
    all_gather x1, waiting for transfers between devices, local(): full_rows = lax.all_gather(joined, 'dp', axis=0, tiled=True)  68.9 us
    unnamed x8, starting transfers between devices  30.1 us
    unnamed x62, local copies, waits for them, and re-layouts  10.2 us
  transfers between devices with their start and end apart: 10, of which 2 were waited for; matrix products, arithmetic and copies ran while one was open for 3% of the time, Pallas kernels for 0%

commit v1 on v0

v1 whole, which is shorter than its diff:
```python
import functools
import math

import jax
import jax.numpy as jnp
import numpy as np
from jax import lax
from jax.experimental import pallas as pl
from jax.experimental.pallas import tpu as pltpu
from jax.sharding import PartitionSpec as P

SEQUENCE_LENGTH = 256

norm_eps = 1e-06
beta_one = 0.9
beta_two = 0.999
adam_eps = 1e-08
learn_rate = 0.01
decay_rate = 0.1
bias_one = 1.0 - 0.9**2
bias_two = 1.0 - 0.999**2

MESH = pl.DeviceIdType.MESH
BF16 = jnp.bfloat16
F32 = jnp.float32

Y_SIZE = 8
CHIPS = 16
HEAD_RANKS = 16
LANES = 640
CHUNK = 16
SLOT = 32
VMEM_SPEC = pl.BlockSpec(memory_space=pltpu.VMEM)


def angle_tables(rope_width):
    half_width = rope_width // 2
    inverse_freq = np.exp(
        np.arange(half_width, dtype=np.float32)
        * np.float32(-2.0 * math.log(10000.0) / rope_width)
    ).astype(np.float32)
    angles = np.arange(SEQUENCE_LENGTH, dtype=np.float32)[:, None] * inverse_freq[None, :]
    return np.cos(angles).astype(np.float32), np.sin(angles).astype(np.float32)


def gather_kernel(
    key_ref, value_ref, key_out, value_out,
    y_send, y_recv, x_send, x_recv, c_send, c_recv, own_sem,
):
    dp = lax.axis_index("dp")
    core = lax.rem(dp, 2)
    chip = dp // 2
    y_pos = lax.rem(chip, Y_SIZE)
    x_pos = chip // Y_SIZE

    def place(x, y, c):
        return (x * Y_SIZE + lax.rem(y + Y_SIZE, Y_SIZE)) * 2 + c

    other_x = 1 - x_pos
    ups = (place(x_pos, y_pos + 1, core), place(x_pos, y_pos - 1, core))
    x_partner = place(other_x, y_pos, core)
    c_partner = place(x_pos, y_pos, 1 - core)

    barrier = pltpu.get_barrier_semaphore()
    for peer in (ups[0], ups[1], x_partner, c_partner):
        pl.semaphore_signal(barrier, inc=1, device_id={"dp": peer}, device_id_type=MESH)
    pl.semaphore_wait(barrier, 4)

    rows_in = key_ref.shape[0]
    sources = (key_ref, value_ref)
    outs = (key_out, value_out)

    def rows_of(index):
        return pl.ds(pl.multiple_of(index * rows_in, rows_in), rows_in)

    def send(w, src, block, sems, e, peer):
        copy = pltpu.make_async_remote_copy(
            src_ref=src,
            dst_ref=outs[w].at[rows_of(block)],
            send_sem=sems[0].at[e],
            recv_sem=sems[1].at[e],
            device_id={"dp": peer},
            device_id_type=MESH,
        )
        copy.start()
        return copy

    y_sems, x_sems, c_sems = (y_send, y_recv), (x_send, x_recv), (c_send, c_recv)
    steps = {(0, 0): 4, (0, 1): 3, (1, 0): 3, (1, 1): 4}
    event = {}
    for s in range(1, 5):
        for p in range(2):
            for w in range(2):
                for d in range(2):
                    if s <= steps[(w, d)]:
                        event[(s, p, w, d)] = len(event)
    y_copies, x_copies, c_copies = {}, {}, {}

    for w in range(2):
        x_copies[w] = send(w, sources[w], dp, x_sems, w, x_partner)
    for w in range(2):
        for d in range(2):
            e = event[(1, 0, w, d)]
            y_copies[e] = send(w, sources[w], dp, y_sems, e, ups[d])
    for w in range(2):
        c_copies[w] = send(w, sources[w], dp, c_sems, w, c_partner)
    own = []
    for w in range(2):
        copy = pltpu.make_async_copy(sources[w], outs[w].at[rows_of(dp)], own_sem.at[w])
        copy.start()
        own.append(copy)
    for w in range(2):
        x_copies[w].wait_recv()
        view = outs[w].at[rows_of(x_partner)]
        for d in range(2):
            e = event[(1, 1, w, d)]
            y_copies[e] = send(w, view, x_partner, y_sems, e, ups[d])
        c_copies[2 + w] = send(w, view, x_partner, c_sems, 2 + w, c_partner)
    for (s, p, w, d), e in event.items():
        x = x_pos if p == 0 else other_x
        block = place(x, y_pos - s if d == 0 else y_pos + s, core)
        y_copies[e].wait_recv()
        view = outs[w].at[rows_of(block)]
        if s < steps[(w, d)]:
            n = event[(s + 1, p, w, d)]
            y_copies[n] = send(w, view, block, y_sems, n, ups[d])
        c_copies[4 + e] = send(w, view, block, c_sems, 4 + e, c_partner)
    for copy in own:
        copy.wait()
    for copy in x_copies.values():
        copy.wait_send()
    for copy in y_copies.values():
        copy.wait_send()
    for copy in c_copies.values():
        copy.wait()


def gather_up(key_up, value_up, dp_size):
    rows, cols = key_up.shape
    full = jax.ShapeDtypeStruct((rows * dp_size, cols), key_up.dtype)
    dma = pltpu.SemaphoreType.DMA
    return pl.pallas_call(
        gather_kernel,
        out_shape=(full, full),
        in_specs=[VMEM_SPEC] * 2,
        out_specs=(VMEM_SPEC, VMEM_SPEC),
        scratch_shapes=[
            dma((28,)), dma((28,)), dma((2,)), dma((2,)), dma((32,)), dma((32,)), dma((2,)),
        ],
        compiler_params=pltpu.CompilerParams(collective_id=0, has_side_effects=True),
        name="gather_up",
    )(key_up, value_up)


def dot(a, b, dims):
    return lax.dot_general(a, b, (dims, ((), ())), preferred_element_type=F32)


NN = ((1,), (0,))
NT = ((1,), (1,))
TN = ((0,), (0,))


def attention_kernel(
    scale_factor,
    latent_ref, raw_ref, gain_ref, cos_ref, sin_ref,
    query_ref, rope_ref, cot_ref, key_up_ref, value_up_ref,
    grad_query_ref, grad_rope_ref, part_ref,
    latent, key_rot, total, rope_total,
):
    step = pl.program_id(0)
    rank = latent_ref.shape[1]
    rope_width = raw_ref.shape[1]
    half = rope_width // 2

    @pl.when(step == 0)
    def _():
        x = latent_ref[...].astype(F32)
        inv = lax.rsqrt(jnp.mean(x * x, axis=1, keepdims=True) + norm_eps)
        latent[...] = (x * inv * gain_ref[...]).astype(BF16)
        raw = raw_ref[...].astype(F32)
        u, w = raw[:, :half], raw[:, half:]
        cos, sin = cos_ref[...], sin_ref[...]
        key_rot[...] = jnp.concatenate((u * cos - w * sin, u * sin + w * cos), axis=1).astype(BF16)
        total[...] = jnp.zeros_like(total)
        rope_total[...] = jnp.zeros_like(rope_total)

    tokens = latent_ref.shape[0]
    width = query_ref.shape[1] // 2
    keys2 = dot(latent[...], key_up_ref[...], NN).astype(BF16)
    values2 = dot(latent[...], value_up_ref[...], NN).astype(BF16)
    rot = key_rot[...]
    causal = lax.broadcasted_iota(jnp.int32, (tokens, tokens), 0) >= lax.broadcasted_iota(
        jnp.int32, (tokens, tokens), 1
    )
    grad_keys, grad_values, grad_ropes = [], [], []
    for h in range(2):
        cols = slice(h * width, (h + 1) * width)
        query = query_ref[:, cols]
        rope = rope_ref[:, h * rope_width : (h + 1) * rope_width]
        cot = cot_ref[:, cols]
        key = keys2[:, cols]
        value = values2[:, cols]
        scores = (dot(query, key, NT) + dot(rope, rot, NT)) * scale_factor
        scores = jnp.where(causal, scores, -1e30)
        grown = jnp.exp(scores - jnp.max(scores, axis=1, keepdims=True))
        probs = grown / jnp.sum(grown, axis=1, keepdims=True)
        prob_low = probs.astype(BF16)
        grad_probs = dot(cot, value, NT)
        delta = jnp.sum(prob_low.astype(F32) * grad_probs, axis=1, keepdims=True)
        score_low = (probs * (grad_probs - delta) * scale_factor).astype(BF16)
        grad_query_ref[:, cols] = dot(score_low, key, NN).astype(BF16)
        grad_ropes.append(dot(score_low, rot, NN).astype(BF16))
        grad_keys.append(dot(score_low, query, TN).astype(BF16))
        grad_values.append(dot(prob_low, cot, TN).astype(BF16))
        rope_total[...] += dot(score_low, rope, TN)
    grad_rope_ref[...] = jnp.concatenate(grad_ropes, axis=1)
    total[...] += dot(jnp.concatenate(grad_keys, axis=1), key_up_ref[...], NT) + dot(
        jnp.concatenate(grad_values, axis=1), value_up_ref[...], NT
    )

    @pl.when(step == pl.num_programs(0) - 1)
    def _():
        part_ref[:, :rank] = total[...].astype(BF16)
        part_ref[:, rank:] = jnp.concatenate(
            (rope_total[...], jnp.zeros((tokens, LANES - rank - rope_width), F32)), axis=1
        ).astype(BF16)


def attention_back(latent_in, raw_key, gain, cos, sin, query, rope, cot, key_full, value_full):
    tokens, rank = latent_in.shape
    rope_width = raw_key.shape[1]
    heads = rope.shape[1] // rope_width
    width = query.shape[1] // heads
    whole = lambda a: pl.BlockSpec(a.shape, lambda i: (0, 0))
    cut = lambda rows, cols: pl.BlockSpec((rows, cols), lambda i: (0, i))
    scale_factor = 1.0 / math.sqrt(width + rope_width)
    return pl.pallas_call(
        functools.partial(attention_kernel, scale_factor),
        grid=(heads // 2,),
        out_shape=(
            jax.ShapeDtypeStruct(query.shape, BF16),
            jax.ShapeDtypeStruct(rope.shape, BF16),
            jax.ShapeDtypeStruct((tokens, LANES), BF16),
        ),
        in_specs=[
            whole(latent_in), whole(raw_key), whole(gain), whole(cos), whole(sin),
            cut(tokens, 2 * width), cut(tokens, 2 * rope_width), cut(tokens, 2 * width),
            cut(rank, 2 * width), cut(rank, 2 * width),
        ],
        out_specs=(
            cut(tokens, 2 * width),
            cut(tokens, 2 * rope_width),
            pl.BlockSpec((tokens, LANES), lambda i: (0, 0)),
        ),
        scratch_shapes=[
            pltpu.VMEM((tokens, rank), BF16),
            pltpu.VMEM((tokens, rope_width), BF16),
            pltpu.VMEM((tokens, rank), F32),
            pltpu.VMEM((tokens, rope_width), F32),
        ],
        name="attention_back",
    )(latent_in, raw_key, gain, cos, sin, query, rope, cot, key_full, value_full)


def tail_kernel(
    part_ref, latent_ref, gain_ref, cos_ref, sin_ref, hidden_ref, out_ref,
    sum_recv, kv_own, kv_all, wide, core_out, core_in, chip_out, chip_in,
    s1, r1, s2, r2, s3, r3, s4, r4,
):
    dp = lax.axis_index("dp")
    head = lax.axis_index("head")
    core = lax.rem(dp, 2)
    chip = dp // 2
    rank = latent_ref.shape[1]
    rope_width = 2 * cos_ref.shape[1]
    half = rope_width // 2
    rows_out = out_ref.shape[0]
    kv_width = rank + rope_width

    def head_peer(k):
        return lax.rem(head + k, HEAD_RANKS)

    def chip_peer(k):
        return lax.rem(chip + k, CHIPS)

    barrier = pltpu.get_barrier_semaphore()

    @pl.loop(1, HEAD_RANKS)
    def _(k):
        pl.semaphore_signal(barrier, inc=1, device_id={"head": head_peer(k)}, device_id_type=MESH)

    @pl.loop(1, CHIPS)
    def _(k):
        pl.semaphore_signal(
            barrier, inc=1, device_id={"dp": chip_peer(k) * 2 + core}, device_id_type=MESH
        )

    core_peer = chip * 2 + 1 - core
    pl.semaphore_signal(barrier, inc=1, device_id={"dp": core_peer}, device_id_type=MESH)
    pl.semaphore_wait(barrier, HEAD_RANKS - 1 + CHIPS - 1 + 1)

    def rows_of(index, size):
        return pl.ds(pl.multiple_of(index * size, size), size)

    def sum_copy(k):
        return pltpu.make_async_remote_copy(
            src_ref=part_ref.at[rows_of(head_peer(k), CHUNK)],
            dst_ref=sum_recv.at[k],
            send_sem=s1.at[k],
            recv_sem=r1.at[k],
            device_id={"head": head_peer(k)},
            device_id_type=MESH,
        )

    @pl.loop(1, HEAD_RANKS)
    def _(k):
        sum_copy(k).start()

    mine = rows_of(head, CHUNK)
    x = latent_ref[mine, :].astype(F32)
    inv = lax.rsqrt(jnp.mean(x * x, axis=1, keepdims=True) + norm_eps)
    cos, sin = cos_ref[mine, :], sin_ref[mine, :]
    total = part_ref[mine, :].astype(F32)

    @pl.loop(1, HEAD_RANKS)
    def _(k):
        sum_copy(k).wait()

    for k in range(1, HEAD_RANKS):
        total += sum_recv[k].astype(F32)
    scaled = gain_ref[...] * total[:, :rank]
    inner = jnp.sum(x * scaled, axis=1, keepdims=True)
    latent_grad = inv * scaled - x * (inv * inv * inv) * inner / rank
    g, q = total[:, rank : rank + half], total[:, rank + half : rank + rope_width]
    tail = jnp.concatenate(
        (
            g * cos + q * sin,
            q * cos - g * sin,
            jnp.zeros((CHUNK, LANES - kv_width), F32),
        ),
        axis=1,
    )
    kv_own[:, :rank] = latent_grad.astype(BF16)
    kv_own[:, rank:] = tail.astype(BF16)

    def kv_copy(k):
        return pltpu.make_async_remote_copy(
            src_ref=kv_own,
            dst_ref=kv_all.at[mine],
            send_sem=s2.at[k],
            recv_sem=r2.at[k],
            device_id={"head": head_peer(k)},
            device_id_type=MESH,
        )

    @pl.loop(1, HEAD_RANKS)
    def _(k):
        kv_copy(k).start()

    kv_all[mine, :] = kv_own[...]

    row = lax.broadcasted_iota(jnp.int32, (2 * CHIPS * SLOT, 1), 0)
    r = row % SLOT
    owner = row // SLOT
    source = ((owner % CHIPS) * 2 + owner // CHIPS) * rows_out + r
    source = jnp.where(r < rows_out, source, -1)
    column = lax.broadcasted_iota(jnp.int32, (2 * CHIPS * SLOT, LANES), 1)
    pick = jnp.where(column == source, 1.0, 0.0).astype(BF16)

    @pl.loop(1, HEAD_RANKS)
    def _(k):
        kv_copy(k).wait()

    picked = dot(pick, kv_all[...], NT).astype(BF16)
    wide[...] = dot(picked, hidden_ref[...], NN)

    span = CHIPS * SLOT
    core_out[...] = wide[rows_of(1 - core, span), :].astype(BF16)
    core_copy = pltpu.make_async_remote_copy(
        src_ref=core_out,
        dst_ref=core_in,
        send_sem=s3,
        recv_sem=r3,
        device_id={"dp": core_peer},
        device_id_type=MESH,
    )
    core_copy.start()
    core_copy.wait()
    chip_out[...] = (wide[rows_of(core, span), :] + core_in[...].astype(F32)).astype(BF16)

    def chip_copy(k):
        return pltpu.make_async_remote_copy(
            src_ref=chip_out.at[rows_of(chip_peer(k), SLOT)],
            dst_ref=chip_in.at[k],
            send_sem=s4.at[k],
            recv_sem=r4.at[k],
            device_id={"dp": chip_peer(k) * 2 + core},
            device_id_type=MESH,
        )

    @pl.loop(1, CHIPS)
    def _(k):
        chip_copy(k).start()

    own_rows = rows_of(chip, SLOT)
    first = wide[rows_of(core * CHIPS + chip, SLOT), :] + core_in[own_rows, :].astype(F32)

    @pl.loop(1, CHIPS)
    def _(k):
        chip_copy(k).wait()

    for k in range(1, CHIPS):
        first += chip_in[k].astype(F32)
    out_ref[...] = first[:rows_out, :]


def tail(part, latent_in, gain, cos, sin, hidden, rows_out):
    cols = hidden.shape[1]
    tokens = hidden.shape[0]
    dma = pltpu.SemaphoreType.DMA
    span = CHIPS * SLOT
    return pl.pallas_call(
        tail_kernel,
        out_shape=jax.ShapeDtypeStruct((rows_out, cols), F32),
        in_specs=[VMEM_SPEC] * 6,
        out_specs=VMEM_SPEC,
        scratch_shapes=[
            pltpu.VMEM((HEAD_RANKS, CHUNK, LANES), BF16),
            pltpu.VMEM((CHUNK, LANES), BF16),
            pltpu.VMEM((tokens, LANES), BF16),
            pltpu.VMEM((2 * span, cols), F32),
            pltpu.VMEM((span, cols), BF16),
            pltpu.VMEM((span, cols), BF16),
            pltpu.VMEM((span, cols), BF16),
            pltpu.VMEM((CHIPS, SLOT, cols), BF16),
            dma((HEAD_RANKS,)), dma((HEAD_RANKS,)), dma((HEAD_RANKS,)), dma((HEAD_RANKS,)),
            dma, dma, dma((CHIPS,)), dma((CHIPS,)),
        ],
        compiler_params=pltpu.CompilerParams(collective_id=1, has_side_effects=True),
        name="tail",
    )(part, latent_in, gain, cos, sin, hidden)


def local(
    hidden_in,
    latent_unnormed,
    unrotated_key,
    latent_norm_scale,
    plain_query_rows,
    rotated_query_rows,
    key_up_matrix,
    value_up_matrix,
    output_cotangent,
    down_weight,
    first_moment,
    second_moment,
):
    row_count = latent_unnormed.shape[0]
    dp_size = lax.axis_size("dp")
    cos, sin = angle_tables(unrotated_key.shape[1])
    cos, sin = jnp.asarray(cos), jnp.asarray(sin)
    gain = latent_norm_scale[None, :]
    key_full, value_full = gather_up(key_up_matrix, value_up_matrix, dp_size)
    grad_query, grad_rope, part = attention_back(
        latent_unnormed, unrotated_key, gain, cos, sin,
        plain_query_rows, rotated_query_rows, output_cotangent, key_full, value_full,
    )
    weight_sum = tail(
        part, latent_unnormed, gain, cos, sin, hidden_in, down_weight.shape[0]
    )
    weight_grad = weight_sum / (row_count * dp_size)
    new_first = beta_one * first_moment + (1.0 - beta_one) * weight_grad
    new_second = beta_two * second_moment + (1.0 - beta_two) * weight_grad * weight_grad
    direction = new_first / bias_one / (jnp.sqrt(new_second / bias_two) + adam_eps)
    new_weight = down_weight - learn_rate * (direction + decay_rate * down_weight)
    return grad_query, grad_rope, new_weight, new_first, new_second


def solution(mesh):
    placed = (
        P("dp", "head"),
        P("dp", None),
        P("dp", None),
        P(),
        P("dp", "head"),
        P("dp", "head"),
        P("dp", "head"),
        P("dp", "head"),
        P("dp", "head"),
        P("dp", "head"),
        P("dp", "head"),
        P("dp", "head"),
    )
    return jax.shard_map(
        local,
        mesh=mesh,
        in_specs=placed,
        out_specs=(
            P("dp", "head"),
            P("dp", "head"),
            P("dp", "head"),
            P("dp", "head"),
            P("dp", "head"),
        ),
        check_vma=False,
    )
```

time: 379 us -> 95.1 us (0.25)
  waiting for transfers between devices: 221 us -> 0 us
  Pallas kernels: 0 us -> 90.9 us
  blocking collectives: 71.5 us -> 0 us
  starting transfers between devices: 30.2 us -> 0 us
  local copies, waits for them, and re-layouts: 16.7 us -> 1.58 us
  between operations: 15.2 us -> 0.7 us
  matrix products: 12.2 us -> 0 us
  other arithmetic: 9.68 us -> 1.47 us
    psum x1 -> x0, waiting for transfers between devices: 152 us -> none  [local(): latent_sum, rope_sum = lax.psum((latent_part, rope_part), 'head')]
    pallas_call x0 -> x3, Pallas kernels: none -> 90.9 us  [the longest x1 51.9 us: tail(): pl.pallas_call(tail_kernel, out_shape=jax.ShapeDtypeStruct((rows_out, col...]
    unnamed x1 -> x0, blocking collectives: 71.5 us -> none
    all_gather x1 -> x0, waiting for transfers between devices: 68.9 us -> none  [local(): full_rows = lax.all_gather(joined, 'dp', axis=0, tiled=True)]
    unnamed x8 -> x0, starting transfers between devices: 30.1 us -> none
    dot_general x12 -> x0, matrix products: 12.2 us -> none  [the longest x1 2.35 us: local(): projected = jnp.dot(latent, full_rows, preferred_element_type=jnp.float32)]
    unnamed x62 -> x12, local copies, waits for them, and re-layouts: 10.2 us -> 1.58 us
  transfers between devices with their start and end apart: 10 -> 0, of which waited for: 2 -> 0; matrix products, arithmetic and copies ran while one was open for 3% -> 0% of each run, Pallas kernels for 0% -> 0%
where the time goes in v1:
time: 95.1 us; the launch traced here: 94.7 us
  Pallas kernels  90.9 us (96%)
  local copies, waits for them, and re-layouts  1.58 us (2%)
  other arithmetic  1.47 us (2%)
    pallas_call x1, Pallas kernels, tail(): pl.pallas_call(tail_kernel, out_shape=jax.ShapeDtypeStruct((rows_out, col...  51.9 us
    pallas_call x1, Pallas kernels, gather_up(): pl.pallas_call(gather_kernel, out_shape=(full, full), in_specs=[VMEM_SPEC...  28.4 us
    pallas_call x1, Pallas kernels, attention_back(): pl.pallas_call(functools.partial(attention_kernel, scale_factor), grid=(h...  10.6 us

profile of v1, /device:TPU:1, one launch (start us, length us, event | category | flops | bytes accessed | tf_op | source)
XLA Modules:
  0.0 94.7 jit_solution(14914347764751447251)
XLA Ops:
  0.6 0.0 copy-start.4
  0.6 28.4 %gather_up.1 = (bf16[512,1024]{1,0:T(8,128)(2,1)}, bf16[512,1024]{1,0:T(8,128)(2,1)}) custom-call(bf16[16,1024]{1,0:T(8,128)(2,1)} %key_ref.1, bf16[16,1024]{1,0:T(8,128)(2,1)} %value_ref.1), custom_call_target="tpu_custom_call" | custom-call | tf_op jit(solution)/shard_map/gather_up/pallas_call | solution.py:142
  29.0 0.0 copy-done.4
  29.0 0.7 copy.19.raw_ref
  29.8 0.0 copy-start
  29.8 10.6 %attention_back.1 = (bf16[256,1024]{1,0:T(8,128)(2,1)}, bf16[256,512]{1,0:T(8,128)(2,1)}, bf16[256,640]{1,0:T(8,128)(2,1)}) custom-call(bf16[256,512]{1,0:T(8,128)(2,1)} %latent_ref.3, bf16[256,64]{1,0:T(8,128)(2,1)} %copy.19.raw_ref, f32[1,512]{1,0:T(1,128)} %bitcast.1, f32[256,32]{1,0:T(8,128)} %constant.28.clone.cos_ref, ...), custom_call_target="tpu_custom_call" | custom-call | tf_op jit(solution)/shard_map/attention_back/pallas_call | solution.py:238
  40.4 0.0 copy-done
  40.4 0.8 copy.20.hidden_ref
  41.2 0.0 copy-start.1
  41.2 0.0 copy-start.2
  41.2 0.0 copy-start.3
  41.2 51.9 %tail.1 = f32[18,448]{1,0:T(8,128)} custom-call(bf16[256,640]{1,0:T(8,128)(2,1)} %get-tuple-element.14.part_ref, bf16[256,512]{1,0:T(8,128)(2,1)} %latent_ref.3, f32[1,512]{1,0:T(1,128)} %bitcast.2, f32[256,32]{1,0:T(8,128)} %constant.28.clone.cos_ref, f32[256,32]{1,0:T(8,128)} %constant.29.clone.sin_ref, bf16[256,448]{1,0:T(8,128)(2,1)} %copy.20.hidden_ref), custom_call_target="tpu_custom_call" | custom-call | tf_op jit(solution)/shard_map/tail/pallas_call | solution.py:423
  93.2 0.0 copy-done.1
  93.2 0.0 copy-done.2
  93.2 0.0 copy-done.3
  93.2 1.5 %multiply_subtract_fusion = (f32[18,448]{1,0:T(8,128)}, f32[18,448]{1,0:T(8,128)}, f32[18,448]{1,0:T(8,128)}) fusion(f32[18,448]{1,0:T(8,128)S(1)} %copy-done.1, f32[18,448]{1,0:T(8,128)} %tail.1, f32[18,448]{1,0:T(8,128)S(1)} %copy-done.2, f32[18,448]{1,0:T(8,128)S(1)} %copy-done.3), kind=kLoop, calls=%fused_computation | loop fusion | flops 129024 | bytes 225792 | tf_op jit(solution)/shard_map/sub | solution.py:476
Async XLA Ops:
  0.6 28.4 %copy-start.4 = (bf16[256,64]{0,1:T(8,128)(2,1)S(1)}, bf16[256,64]{0,1:T(8,128)(2,1)}, u32[]{:S(2)}) copy-start(bf16[256,64]{0,1:T(8,128)(2,1)} %param.16) | copy-start | bytes 98308
  29.8 10.6 %copy-start = (bf16[256,448]{0,1:T(8,128)(2,1)S(1)}, bf16[256,448]{0,1:T(8,128)(2,1)}, u32[]{:S(2)}) copy-start(bf16[256,448]{0,1:T(8,128)(2,1)} %param.14) | copy-start | bytes 688132
  41.2 51.9 %copy-start.1 = (f32[18,448]{1,0:T(8,128)S(1)}, f32[18,448]{1,0:T(8,128)}, u32[]{:S(2)}) copy-start(f32[18,448]{1,0:T(8,128)} %param.23) | copy-start | bytes 96772
  41.2 51.9 %copy-start.2 = (f32[18,448]{1,0:T(8,128)S(1)}, f32[18,448]{1,0:T(8,128)}, u32[]{:S(2)}) copy-start(f32[18,448]{1,0:T(8,128)} %param.24) | copy-start | bytes 96772
  41.2 51.9 %copy-start.3 = (f32[18,448]{1,0:T(8,128)S(1)}, f32[18,448]{1,0:T(8,128)}, u32[]{:S(2)}) copy-start(f32[18,448]{1,0:T(8,128)} %param.25) | copy-start | bytes 96772

commit v2 on v1

--- a/solution.py
+++ b/solution.py
@@ -25,11 +25,11 @@
 F32 = jnp.float32
 
 Y_SIZE = 8
-CHIPS = 16
 HEAD_RANKS = 16
 LANES = 640
 CHUNK = 16
-SLOT = 32
+SLOT = 24
+QUAD = 4
 VMEM_SPEC = pl.BlockSpec(memory_space=pltpu.VMEM)
 
 
@@ -44,8 +44,8 @@
 
 
 def gather_kernel(
-    key_ref, value_ref, key_out, value_out,
-    y_send, y_recv, x_send, x_recv, c_send, c_recv, own_sem,
+    key_ref, value_ref, hidden_ref, key_out, value_out, hidden_out,
+    y_send, y_recv, x_send, x_recv, c_send, c_recv, own_sem, h_send, h_recv,
 ):
     dp = lax.axis_index("dp")
     core = lax.rem(dp, 2)
@@ -109,6 +109,27 @@
         copy = pltpu.make_async_copy(sources[w], outs[w].at[rows_of(dp)], own_sem.at[w])
         copy.start()
         own.append(copy)
+    def hidden_rows(x, c):
+        size = hidden_ref.shape[0]
+        return hidden_out.at[pl.ds(pl.multiple_of((x * 2 + c) * size, size), size)]
+
+    def send_hidden(src, dst, e, peer):
+        copy = pltpu.make_async_remote_copy(
+            src_ref=src,
+            dst_ref=dst,
+            send_sem=h_send.at[e],
+            recv_sem=h_recv.at[e],
+            device_id={"dp": peer},
+            device_id_type=MESH,
+        )
+        copy.start()
+        return copy
+
+    hidden_x = send_hidden(hidden_ref, hidden_rows(x_pos, core), 0, x_partner)
+    hidden_c = send_hidden(hidden_ref, hidden_rows(x_pos, core), 1, c_partner)
+    copy = pltpu.make_async_copy(hidden_ref, hidden_rows(x_pos, core), own_sem.at[2])
+    copy.start()
+    own.append(copy)
     for w in range(2):
         x_copies[w].wait_recv()
         view = outs[w].at[rows_of(x_partner)]
@@ -125,6 +146,9 @@
             n = event[(s + 1, p, w, d)]
             y_copies[n] = send(w, view, block, y_sems, n, ups[d])
         c_copies[4 + e] = send(w, view, block, c_sems, 4 + e, c_partner)
+    hidden_x.wait_recv()
+    far = hidden_rows(other_x, core)
+    hidden_d = send_hidden(far, far, 2, c_partner)
     for copy in own:
         copy.wait()
     for copy in x_copies.values():
@@ -133,23 +157,29 @@
         copy.wait_send()
     for copy in c_copies.values():
         copy.wait()
-
-
-def gather_up(key_up, value_up, dp_size):
+    hidden_x.wait_send()
+    hidden_c.wait()
+    hidden_d.wait()
+
+
+def gather_up(key_up, value_up, hidden, dp_size):
     rows, cols = key_up.shape
     full = jax.ShapeDtypeStruct((rows * dp_size, cols), key_up.dtype)
     dma = pltpu.SemaphoreType.DMA
     return pl.pallas_call(
         gather_kernel,
-        out_shape=(full, full),
-        in_specs=[VMEM_SPEC] * 2,
-        out_specs=(VMEM_SPEC, VMEM_SPEC),
+        out_shape=(
+            full, full, jax.ShapeDtypeStruct((QUAD * hidden.shape[0], hidden.shape[1]), BF16)
+        ),
+        in_specs=[VMEM_SPEC] * 3,
+        out_specs=(VMEM_SPEC,) * 3,
         scratch_shapes=[
-            dma((28,)), dma((28,)), dma((2,)), dma((2,)), dma((32,)), dma((32,)), dma((2,)),
+            dma((28,)), dma((28,)), dma((2,)), dma((2,)), dma((32,)), dma((32,)), dma((3,)),
+            dma((3,)), dma((3,)),
         ],
         compiler_params=pltpu.CompilerParams(collective_id=0, has_side_effects=True),
         name="gather_up",
-    )(key_up, value_up)
+    )(key_up, value_up, hidden)
 
 
 def dot(a, b, dims):
@@ -221,10 +251,10 @@
 
     @pl.when(step == pl.num_programs(0) - 1)
     def _():
-        part_ref[:, :rank] = total[...].astype(BF16)
+        part_ref[:, :rank] = total[...]
         part_ref[:, rank:] = jnp.concatenate(
             (rope_total[...], jnp.zeros((tokens, LANES - rank - rope_width), F32)), axis=1
-        ).astype(BF16)
+        )
 
 
 def attention_back(latent_in, raw_key, gain, cos, sin, query, rope, cot, key_full, value_full):
@@ -241,7 +271,7 @@
         out_shape=(
             jax.ShapeDtypeStruct(query.shape, BF16),
             jax.ShapeDtypeStruct(rope.shape, BF16),
-            jax.ShapeDtypeStruct((tokens, LANES), BF16),
+            jax.ShapeDtypeStruct((tokens, LANES), F32),
         ),
         in_specs=[
             whole(latent_in), whole(raw_key), whole(gain), whole(cos), whole(sin),
@@ -263,26 +293,60 @@
     )(latent_in, raw_key, gain, cos, sin, query, rope, cot, key_full, value_full)
 
 
+def tail_tables(rows_out):
+    per_quad = Y_SIZE * rows_out
+
+    def column(member, q):
+        y, r = divmod(q, rows_out)
+        return (((member // 2) * Y_SIZE + y) * 2 + member % 2) * rows_out + r
+
+    extra = per_quad - 128
+    order = np.full((1, (QUAD + 1) * 128), -1, np.int32)
+    for member in range(QUAD):
+        for q in range(per_quad):
+            lane = member * 128 + q if q < 128 else QUAD * 128 + member * extra + q - 128
+            order[0, lane] = column(member, q)
+    rows = np.full((Y_SIZE * SLOT, 1), -1000, np.int32)
+    for y in range(Y_SIZE):
+        rows[y * SLOT : y * SLOT + rows_out, 0] = y * rows_out + np.arange(rows_out)
+    return order, rows
+
+
 def tail_kernel(
-    part_ref, latent_ref, gain_ref, cos_ref, sin_ref, hidden_ref, out_ref,
-    sum_recv, kv_own, kv_all, wide, core_out, core_in, chip_out, chip_in,
+    part_ref, latent_ref, gain_ref, cos_ref, sin_ref, hidden_ref, order_ref, rows_ref, out_ref,
+    sum_recv, kv_own, quad_out, quad_in, block_out, block_all, y_out, y_in,
     s1, r1, s2, r2, s3, r3, s4, r4,
 ):
     dp = lax.axis_index("dp")
     head = lax.axis_index("head")
     core = lax.rem(dp, 2)
     chip = dp // 2
+    y_pos = lax.rem(chip, Y_SIZE)
+    x_pos = chip // Y_SIZE
+    member = x_pos * 2 + core
     rank = latent_ref.shape[1]
+    tokens = latent_ref.shape[0]
     rope_width = 2 * cos_ref.shape[1]
     half = rope_width // 2
     rows_out = out_ref.shape[0]
     kv_width = rank + rope_width
+    extra = Y_SIZE * rows_out - 128
 
     def head_peer(k):
         return lax.rem(head + k, HEAD_RANKS)
 
-    def chip_peer(k):
-        return lax.rem(chip + k, CHIPS)
+    def y_peer(k):
+        return lax.rem(y_pos + k, Y_SIZE)
+
+    def y_device(k):
+        return (x_pos * Y_SIZE + y_peer(k)) * 2 + core
+
+    def quad_peer(k):
+        return lax.rem(member + k, QUAD)
+
+    def quad_device(k):
+        other = quad_peer(k)
+        return ((other // 2) * Y_SIZE + y_pos) * 2 + lax.rem(other, 2)
 
     barrier = pltpu.get_barrier_semaphore()
 
@@ -290,15 +354,15 @@
     def _(k):
         pl.semaphore_signal(barrier, inc=1, device_id={"head": head_peer(k)}, device_id_type=MESH)
 
-    @pl.loop(1, CHIPS)
-    def _(k):
-        pl.semaphore_signal(
-            barrier, inc=1, device_id={"dp": chip_peer(k) * 2 + core}, device_id_type=MESH
-        )
-
-    core_peer = chip * 2 + 1 - core
-    pl.semaphore_signal(barrier, inc=1, device_id={"dp": core_peer}, device_id_type=MESH)
-    pl.semaphore_wait(barrier, HEAD_RANKS - 1 + CHIPS - 1 + 1)
+    @pl.loop(1, Y_SIZE)
+    def _(k):
+        pl.semaphore_signal(barrier, inc=1, device_id={"dp": y_device(k)}, device_id_type=MESH)
+
+    @pl.loop(1, QUAD)
+    def _(k):
+        pl.semaphore_signal(barrier, inc=1, device_id={"dp": quad_device(k)}, device_id_type=MESH)
+
+    pl.semaphore_wait(barrier, HEAD_RANKS - 1 + Y_SIZE - 1 + QUAD - 1)
 
     def rows_of(index, size):
         return pl.ds(pl.multiple_of(index * size, size), size)
@@ -321,19 +385,21 @@
     x = latent_ref[mine, :].astype(F32)
     inv = lax.rsqrt(jnp.mean(x * x, axis=1, keepdims=True) + norm_eps)
     cos, sin = cos_ref[mine, :], sin_ref[mine, :]
-    total = part_ref[mine, :].astype(F32)
+    total = part_ref[mine, :]
+    iota = lax.broadcasted_iota(jnp.int32, (LANES, LANES), 0)
+    select = jnp.where(iota == order_ref[...], 1.0, 0.0).astype(BF16)
 
     @pl.loop(1, HEAD_RANKS)
     def _(k):
         sum_copy(k).wait()
 
     for k in range(1, HEAD_RANKS):
-        total += sum_recv[k].astype(F32)
+        total += sum_recv[k]
     scaled = gain_ref[...] * total[:, :rank]
     inner = jnp.sum(x * scaled, axis=1, keepdims=True)
     latent_grad = inv * scaled - x * (inv * inv * inv) * inner / rank
     g, q = total[:, rank : rank + half], total[:, rank + half : rank + rope_width]
-    tail = jnp.concatenate(
+    rope_grad = jnp.concatenate(
         (
             g * cos + q * sin,
             q * cos - g * sin,
@@ -342,104 +408,123 @@
         axis=1,
     )
     kv_own[:, :rank] = latent_grad.astype(BF16)
-    kv_own[:, rank:] = tail.astype(BF16)
-
-    def kv_copy(k):
+    kv_own[:, rank:] = rope_grad.astype(BF16)
+
+    sent = dot(kv_own[...], select, NN).astype(BF16)
+    for m in range(QUAD):
+        quad_out[m, 0] = sent[:, m * 128 : (m + 1) * 128]
+        quad_out[m, 1] = sent[:, QUAD * 128 :]
+
+    def quad_copy(k):
         return pltpu.make_async_remote_copy(
-            src_ref=kv_own,
-            dst_ref=kv_all.at[mine],
+            src_ref=quad_out.at[quad_peer(k)],
+            dst_ref=quad_in.at[member],
             send_sem=s2.at[k],
             recv_sem=r2.at[k],
+            device_id={"dp": quad_device(k)},
+            device_id_type=MESH,
+        )
+
+    for k in range(1, QUAD):
+        quad_copy(k).start()
+    quad_in[member] = quad_out[member]
+    lane_in = lax.broadcasted_iota(jnp.int32, (128, 128), 0)
+    lane_to = lax.broadcasted_iota(jnp.int32, (128, 128), 1)
+    for k in range(1, QUAD):
+        quad_copy(k).wait()
+    rest = jnp.zeros((CHUNK, 128), F32)
+    for m in range(QUAD):
+        block_out[m] = quad_in[m, 0]
+        inside = (lane_to >= m * extra) & (lane_to < (m + 1) * extra)
+        move = inside & (lane_in - member * extra == lane_to - m * extra)
+        rest += dot(quad_in[m, 1], jnp.where(move, 1.0, 0.0).astype(BF16), NN)
+    block_out[QUAD] = rest.astype(BF16)
+
+    def block_copy(k):
+        return pltpu.make_async_remote_copy(
+            src_ref=block_out,
+            dst_ref=block_all.at[:, mine],
+            send_sem=s3.at[k],
+            recv_sem=r3.at[k],
             device_id={"head": head_peer(k)},
             device_id_type=MESH,
         )
 
     @pl.loop(1, HEAD_RANKS)
     def _(k):
-        kv_copy(k).start()
-
-    kv_all[mine, :] = kv_own[...]
-
-    row = lax.broadcasted_iota(jnp.int32, (2 * CHIPS * SLOT, 1), 0)
-    r = row % SLOT
-    owner = row // SLOT
-    source = ((owner % CHIPS) * 2 + owner // CHIPS) * rows_out + r
-    source = jnp.where(r < rows_out, source, -1)
-    column = lax.broadcasted_iota(jnp.int32, (2 * CHIPS * SLOT, LANES), 1)
-    pick = jnp.where(column == source, 1.0, 0.0).astype(BF16)
+        block_copy(k).start()
+
+    block_all[:, mine, :] = block_out[...]
+    q_row = rows_ref[...]
+    lane = lax.broadcasted_iota(jnp.int32, (Y_SIZE * SLOT, 128), 1)
+    pick = jnp.where(lane == q_row, 1.0, 0.0).astype(BF16)
+    q_rest = jnp.where(q_row >= 128, q_row - 128, -1000)
+    pick_rest = [
+        jnp.where(lane == q_rest + m * extra, 1.0, 0.0).astype(BF16) for m in range(QUAD)
+    ]
 
     @pl.loop(1, HEAD_RANKS)
     def _(k):
-        kv_copy(k).wait()
-
-    picked = dot(pick, kv_all[...], NT).astype(BF16)
-    wide[...] = dot(picked, hidden_ref[...], NN)
-
-    span = CHIPS * SLOT
-    core_out[...] = wide[rows_of(1 - core, span), :].astype(BF16)
-    core_copy = pltpu.make_async_remote_copy(
-        src_ref=core_out,
-        dst_ref=core_in,
-        send_sem=s3,
-        recv_sem=r3,
-        device_id={"dp": core_peer},
-        device_id_type=MESH,
-    )
-    core_copy.start()
-    core_copy.wait()
-    chip_out[...] = (wide[rows_of(core, span), :] + core_in[...].astype(F32)).astype(BF16)
-
-    def chip_copy(k):
+        block_copy(k).wait()
+
+    grad = jnp.zeros((Y_SIZE * SLOT, hidden_ref.shape[1]), F32)
+    for m in range(QUAD):
+        picked = dot(pick, block_all[m], NT) + dot(pick_rest[m], block_all[QUAD], NT)
+        grad += dot(
+            picked.astype(BF16), hidden_ref[m * tokens : (m + 1) * tokens, :], NN
+        )
+    y_out[...] = grad
+
+    def y_copy(k):
         return pltpu.make_async_remote_copy(
-            src_ref=chip_out.at[rows_of(chip_peer(k), SLOT)],
-            dst_ref=chip_in.at[k],
+            src_ref=y_out.at[rows_of(y_peer(k), SLOT)],
+            dst_ref=y_in.at[k],
             send_sem=s4.at[k],
             recv_sem=r4.at[k],
-            device_id={"dp": chip_peer(k) * 2 + core},
+            device_id={"dp": y_device(k)},
             device_id_type=MESH,
         )
 
-    @pl.loop(1, CHIPS)
-    def _(k):
-        chip_copy(k).start()
-
-    own_rows = rows_of(chip, SLOT)
-    first = wide[rows_of(core * CHIPS + chip, SLOT), :] + core_in[own_rows, :].astype(F32)
-
-    @pl.loop(1, CHIPS)
-    def _(k):
-        chip_copy(k).wait()
-
-    for k in range(1, CHIPS):
-        first += chip_in[k].astype(F32)
+    @pl.loop(1, Y_SIZE)
+    def _(k):
+        y_copy(k).start()
+
+    first = y_out[rows_of(y_pos, SLOT), :]
+
+    @pl.loop(1, Y_SIZE)
+    def _(k):
+        y_copy(k).wait()
+
+    for k in range(1, Y_SIZE):
+        first += y_in[k]
     out_ref[...] = first[:rows_out, :]
 
 
-def tail(part, latent_in, gain, cos, sin, hidden, rows_out):
-    cols = hidden.shape[1]
-    tokens = hidden.shape[0]
+def tail(part, latent_in, gain, cos, sin, hidden_quad, rows_out):
+    tokens = latent_in.shape[0]
+    cols = hidden_quad.shape[1]
     dma = pltpu.SemaphoreType.DMA
-    span = CHIPS * SLOT
+    order, rows = tail_tables(rows_out)
     return pl.pallas_call(
         tail_kernel,
         out_shape=jax.ShapeDtypeStruct((rows_out, cols), F32),
-        in_specs=[VMEM_SPEC] * 6,
+        in_specs=[VMEM_SPEC] * 8,
         out_specs=VMEM_SPEC,
         scratch_shapes=[
-            pltpu.VMEM((HEAD_RANKS, CHUNK, LANES), BF16),
+            pltpu.VMEM((HEAD_RANKS, CHUNK, LANES), F32),
             pltpu.VMEM((CHUNK, LANES), BF16),
-            pltpu.VMEM((tokens, LANES), BF16),
-            pltpu.VMEM((2 * span, cols), F32),
-            pltpu.VMEM((span, cols), BF16),
-            pltpu.VMEM((span, cols), BF16),
-            pltpu.VMEM((span, cols), BF16),
-            pltpu.VMEM((CHIPS, SLOT, cols), BF16),
-            dma((HEAD_RANKS,)), dma((HEAD_RANKS,)), dma((HEAD_RANKS,)), dma((HEAD_RANKS,)),
-            dma, dma, dma((CHIPS,)), dma((CHIPS,)),
+            pltpu.VMEM((QUAD, 2, CHUNK, 128), BF16),
+            pltpu.VMEM((QUAD, 2, CHUNK, 128), BF16),
+            pltpu.VMEM((QUAD + 1, CHUNK, 128), BF16),
+            pltpu.VMEM((QUAD + 1, tokens, 128), BF16),
+            pltpu.VMEM((Y_SIZE * SLOT, cols), F32),
+            pltpu.VMEM((Y_SIZE, SLOT, cols), F32),
+            dma((HEAD_RANKS,)), dma((HEAD_RANKS,)), dma((QUAD,)), dma((QUAD,)),
+            dma((HEAD_RANKS,)), dma((HEAD_RANKS,)), dma((Y_SIZE,)), dma((Y_SIZE,)),
         ],
         compiler_params=pltpu.CompilerParams(collective_id=1, has_side_effects=True),
         name="tail",
-    )(part, latent_in, gain, cos, sin, hidden)
+    )(part, latent_in, gain, cos, sin, hidden_quad, jnp.asarray(order), jnp.asarray(rows))
 
 
 def local(
@@ -461,13 +546,15 @@
     cos, sin = angle_tables(unrotated_key.shape[1])
     cos, sin = jnp.asarray(cos), jnp.asarray(sin)
     gain = latent_norm_scale[None, :]
-    key_full, value_full = gather_up(key_up_matrix, value_up_matrix, dp_size)
+    key_full, value_full, hidden_quad = gather_up(
+        key_up_matrix, value_up_matrix, hidden_in, dp_size
+    )
     grad_query, grad_rope, part = attention_back(
         latent_unnormed, unrotated_key, gain, cos, sin,
         plain_query_rows, rotated_query_rows, output_cotangent, key_full, value_full,
     )
     weight_sum = tail(
-        part, latent_unnormed, gain, cos, sin, hidden_in, down_weight.shape[0]
+        part, latent_unnormed, gain, cos, sin, hidden_quad, down_weight.shape[0]
     )
     weight_grad = weight_sum / (row_count * dp_size)
     new_first = beta_one * first_moment + (1.0 - beta_one) * weight_grad

time: 95.1 us -> 102 us (1.073); the launches traced: 94.7 us -> 100 us
  Pallas kernels: 90.9 us -> 94.7 us
  local copies, waits for them, and re-layouts: 1.58 us -> 3.29 us
    pallas_call x1, Pallas kernels: 51.9 us -> 54.8 us  [tail(): pl.pallas_call(tail_kernel, out_shape=jax.ShapeDtypeStruct((rows_out, col...]
    unnamed x12 -> x8, local copies, waits for them, and re-layouts: 1.58 us -> 3.29 us
where the time goes in v2:
time: 102 us; the launch traced here: 100 us
  Pallas kernels  94.7 us (93%)
  local copies, waits for them, and re-layouts  3.29 us (3%)
  other arithmetic  1.47 us (1%)
    pallas_call x1, Pallas kernels, tail(): pl.pallas_call(tail_kernel, out_shape=jax.ShapeDtypeStruct((rows_out, col...  54.8 us
    pallas_call x1, Pallas kernels, gather_up(): pl.pallas_call(gather_kernel, out_shape=(full, full, jax.ShapeDtypeStruct...  29.2 us
    pallas_call x1, Pallas kernels, attention_back(): pl.pallas_call(functools.partial(attention_kernel, scale_factor), grid=(h...  10.7 us
    unnamed x8, local copies, waits for them, and re-layouts  3.29 us

profile of v2, /device:TPU:1, one launch (start us, length us, event | category | flops | bytes accessed | tf_op | source)
XLA Modules:
  0.0 100.2 jit_solution(7951527967189825917)
XLA Ops:
  0.6 1.5 %copy.22.raw_ref = bf16[256,64]{1,0:T(8,128)(2,1)} copy(bf16[256,64]{0,1:T(8,128)(2,1)} %param.18) | data formatting | bytes 65536 | tf_op args[2]
  2.1 1.8 %copy.21.hidden_ref = bf16[256,448]{1,0:T(8,128)(2,1)} copy(bf16[256,448]{0,1:T(8,128)(2,1)} %param.16) | data formatting | bytes 458752 | tf_op args[0]
  3.9 29.2 %gather_up.1 = (bf16[512,1024]{1,0:T(8,128)(2,1)}, bf16[512,1024]{1,0:T(8,128)(2,1)}, bf16[1024,448]{1,0:T(8,128)(2,1)}) custom-call(bf16[16,1024]{1,0:T(8,128)(2,1)} %key_ref.1, bf16[16,1024]{1,0:T(8,128)(2,1)} %value_ref.1, bf16[256,448]{1,0:T(8,128)(2,1)} %copy.21.hidden_ref), custom_call_target="tpu_custom_call" | custom-call | tf_op jit(solution)/shard_map/gather_up/pallas_call | solution.py:169
  33.1 10.7 %attention_back.1 = (bf16[256,1024]{1,0:T(8,128)(2,1)}, bf16[256,512]{1,0:T(8,128)(2,1)}, f32[256,640]{1,0:T(8,128)}) custom-call(bf16[256,512]{1,0:T(8,128)(2,1)} %latent_ref.3, bf16[256,64]{1,0:T(8,128)(2,1)} %copy.22.raw_ref, f32[1,512]{1,0:T(1,128)} %bitcast.1, f32[256,32]{1,0:T(8,128)} %constant.32.clone.cos_ref, f32[256,32]{1,0:T(8,128)} %constant.33.clone.sin_ref, ...), custom_call_target="tpu_custom_call" | custom-call | tf_op jit(solution)/shard_map/attention_back/pallas_call | solution.py:268
  43.9 0.0 copy-start
  43.9 0.0 copy-start.1
  43.9 0.0 copy-start.2
  43.9 54.8 %tail.1 = f32[18,448]{1,0:T(8,128)} custom-call(f32[256,640]{1,0:T(8,128)} %get-tuple-element.15.part_ref, bf16[256,512]{1,0:T(8,128)(2,1)} %latent_ref.3, f32[1,512]{1,0:T(1,128)} %bitcast.2, f32[256,32]{1,0:T(8,128)} %constant.32.clone.cos_ref, f32[256,32]{1,0:T(8,128)} %constant.33.clone.sin_ref, bf16[1024,448]{1,0:T(8,128)(2,1)} %get-tuple-element.16.hidden_ref, ...), custom_call_target="tpu_custom_call" | custom-call | tf_op jit(solution)/shard_map/tail/pallas_call | solution.py:508
  98.7 0.0 copy-done
  98.7 0.0 copy-done.1
  98.7 0.0 copy-done.2
  98.7 1.5 %multiply_subtract_fusion = (f32[18,448]{1,0:T(8,128)}, f32[18,448]{1,0:T(8,128)}, f32[18,448]{1,0:T(8,128)}) fusion(f32[18,448]{1,0:T(8,128)S(1)} %copy-done, f32[18,448]{1,0:T(8,128)} %tail.1, f32[18,448]{1,0:T(8,128)S(1)} %copy-done.1, f32[18,448]{1,0:T(8,128)S(1)} %copy-done.2), kind=kLoop, calls=%fused_computation | loop fusion | flops 129024 | bytes 225792 | tf_op jit(solution)/shard_map/sub | solution.py:563
Async XLA Ops:
  43.9 54.8 %copy-start = (f32[18,448]{1,0:T(8,128)S(1)}, f32[18,448]{1,0:T(8,128)}, u32[]{:S(2)}) copy-start(f32[18,448]{1,0:T(8,128)} %param.25) | copy-start | bytes 96772
  43.9 54.8 %copy-start.1 = (f32[18,448]{1,0:T(8,128)S(1)}, f32[18,448]{1,0:T(8,128)}, u32[]{:S(2)}) copy-start(f32[18,448]{1,0:T(8,128)} %param.26) | copy-start | bytes 96772
  43.9 54.8 %copy-start.2 = (f32[18,448]{1,0:T(8,128)S(1)}, f32[18,448]{1,0:T(8,128)}, u32[]{:S(2)}) copy-start(f32[18,448]{1,0:T(8,128)} %param.27) | copy-start | bytes 96772

commit v3 on v2

--- a/solution.py
+++ b/solution.py
@@ -29,6 +29,7 @@
 LANES = 640
 CHUNK = 16
 SLOT = 24
+PACKED = 64
 QUAD = 4
 VMEM_SPEC = pl.BlockSpec(memory_space=pltpu.VMEM)
 
@@ -89,11 +90,15 @@
     steps = {(0, 0): 4, (0, 1): 3, (1, 0): 3, (1, 1): 4}
     event = {}
     for s in range(1, 5):
-        for p in range(2):
-            for w in range(2):
-                for d in range(2):
-                    if s <= steps[(w, d)]:
-                        event[(s, p, w, d)] = len(event)
+        for p, w in ((0, 0), (0, 1), (1, 0)):
+            for d in range(2):
+                if s <= steps[(w, d)]:
+                    event[(s, p, w, d)] = len(event)
+    late = {}
+    for s in range(1, 5):
+        for d in range(2):
+            if s <= steps[(1, d)]:
+                late[(s, d)] = len(late)
     y_copies, x_copies, c_copies = {}, {}, {}
 
     for w in range(2):
@@ -133,19 +138,42 @@
     for w in range(2):
         x_copies[w].wait_recv()
         view = outs[w].at[rows_of(x_partner)]
+        if w == 0:
+            for d in range(2):
+                e = event[(1, 1, w, d)]
+                y_copies[e] = send(w, view, x_partner, y_sems, e, ups[d])
+        c_copies[2 + w] = send(w, view, x_partner, c_sems, 2 + w, c_partner)
+
+    def near(s, d):
+        return y_pos - s if d == 0 else y_pos + s
+
+    def take_late(s):
         for d in range(2):
-            e = event[(1, 1, w, d)]
-            y_copies[e] = send(w, view, x_partner, y_sems, e, ups[d])
-        c_copies[2 + w] = send(w, view, x_partner, c_sems, 2 + w, c_partner)
-    for (s, p, w, d), e in event.items():
-        x = x_pos if p == 0 else other_x
-        block = place(x, y_pos - s if d == 0 else y_pos + s, core)
-        y_copies[e].wait_recv()
-        view = outs[w].at[rows_of(block)]
-        if s < steps[(w, d)]:
-            n = event[(s + 1, p, w, d)]
-            y_copies[n] = send(w, view, block, y_sems, n, ups[d])
-        c_copies[4 + e] = send(w, view, block, c_sems, 4 + e, c_partner)
+            if (s, d) in late:
+                e = late[(s, d)]
+                block = place(other_x, near(s, d), core)
+                x_copies[2 + e].wait_recv()
+                view = outs[1].at[rows_of(block)]
+                n = 4 + len(event) + e
+                c_copies[n] = send(1, view, block, c_sems, n, c_partner)
+
+    for s in range(1, 5):
+        for (step, p, w, d), e in event.items():
+            if step != s:
+                continue
+            block = place(x_pos if p == 0 else other_x, near(s, d), core)
+            y_copies[e].wait_recv()
+            view = outs[w].at[rows_of(block)]
+            if s < steps[(w, d)]:
+                n = event[(s + 1, p, w, d)]
+                y_copies[n] = send(w, view, block, y_sems, n, ups[d])
+            if w == 1:
+                n = 2 + late[(s, d)]
+                x_copies[n] = send(w, view, block, x_sems, n, x_partner)
+            c_copies[4 + e] = send(w, view, block, c_sems, 4 + e, c_partner)
+        if s > 1:
+            take_late(s - 1)
+    take_late(4)
     hidden_x.wait_recv()
     far = hidden_rows(other_x, core)
     hidden_d = send_hidden(far, far, 2, c_partner)
@@ -174,7 +202,7 @@
         in_specs=[VMEM_SPEC] * 3,
         out_specs=(VMEM_SPEC,) * 3,
         scratch_shapes=[
-            dma((28,)), dma((28,)), dma((2,)), dma((2,)), dma((32,)), dma((32,)), dma((3,)),
+            dma((21,)), dma((21,)), dma((9,)), dma((9,)), dma((32,)), dma((32,)), dma((3,)),
             dma((3,)), dma((3,)),
         ],
         compiler_params=pltpu.CompilerParams(collective_id=0, has_side_effects=True),
@@ -195,12 +223,12 @@
     scale_factor,
     latent_ref, raw_ref, gain_ref, cos_ref, sin_ref,
     query_ref, rope_ref, cot_ref, key_up_ref, value_up_ref,
-    grad_query_ref, grad_rope_ref, part_ref,
+    grad_query_ref, grad_rope_ref, part_ref, rope_part_ref,
     latent, key_rot, total, rope_total,
 ):
     step = pl.program_id(0)
     rank = latent_ref.shape[1]
-    rope_width = raw_ref.shape[1]
+    rope_width = raw_ref.shape[0]
     half = rope_width // 2
 
     @pl.when(step == 0)
@@ -209,9 +237,9 @@
         inv = lax.rsqrt(jnp.mean(x * x, axis=1, keepdims=True) + norm_eps)
         latent[...] = (x * inv * gain_ref[...]).astype(BF16)
         raw = raw_ref[...].astype(F32)
-        u, w = raw[:, :half], raw[:, half:]
+        u, w = raw[:half], raw[half:]
         cos, sin = cos_ref[...], sin_ref[...]
-        key_rot[...] = jnp.concatenate((u * cos - w * sin, u * sin + w * cos), axis=1).astype(BF16)
+        key_rot[...] = jnp.concatenate((u * cos - w * sin, u * sin + w * cos), axis=0).astype(BF16)
         total[...] = jnp.zeros_like(total)
         rope_total[...] = jnp.zeros_like(rope_total)
 
@@ -231,7 +259,7 @@
         cot = cot_ref[:, cols]
         key = keys2[:, cols]
         value = values2[:, cols]
-        scores = (dot(query, key, NT) + dot(rope, rot, NT)) * scale_factor
+        scores = (dot(query, key, NT) + dot(rope, rot, NN)) * scale_factor
         scores = jnp.where(causal, scores, -1e30)
         grown = jnp.exp(scores - jnp.max(scores, axis=1, keepdims=True))
         probs = grown / jnp.sum(grown, axis=1, keepdims=True)
@@ -240,7 +268,7 @@
         delta = jnp.sum(prob_low.astype(F32) * grad_probs, axis=1, keepdims=True)
         score_low = (probs * (grad_probs - delta) * scale_factor).astype(BF16)
         grad_query_ref[:, cols] = dot(score_low, key, NN).astype(BF16)
-        grad_ropes.append(dot(score_low, rot, NN).astype(BF16))
+        grad_ropes.append(dot(score_low, rot, NT).astype(BF16))
         grad_keys.append(dot(score_low, query, TN).astype(BF16))
         grad_values.append(dot(prob_low, cot, TN).astype(BF16))
         rope_total[...] += dot(score_low, rope, TN)
@@ -251,15 +279,16 @@
 
     @pl.when(step == pl.num_programs(0) - 1)
     def _():
-        part_ref[:, :rank] = total[...]
-        part_ref[:, rank:] = jnp.concatenate(
-            (rope_total[...], jnp.zeros((tokens, LANES - rank - rope_width), F32)), axis=1
+        part_ref[...] = total[...]
+        pairs = rope_total[...].reshape(tokens // CHUNK, 2, CHUNK // 2, rope_width)
+        rope_part_ref[...] = jnp.concatenate((pairs[:, 0], pairs[:, 1]), axis=2).reshape(
+            tokens // 2, 2 * rope_width
         )
 
 
 def attention_back(latent_in, raw_key, gain, cos, sin, query, rope, cot, key_full, value_full):
     tokens, rank = latent_in.shape
-    rope_width = raw_key.shape[1]
+    rope_width = raw_key.shape[0]
     heads = rope.shape[1] // rope_width
     width = query.shape[1] // heads
     whole = lambda a: pl.BlockSpec(a.shape, lambda i: (0, 0))
@@ -271,7 +300,8 @@
         out_shape=(
             jax.ShapeDtypeStruct(query.shape, BF16),
             jax.ShapeDtypeStruct(rope.shape, BF16),
-            jax.ShapeDtypeStruct((tokens, LANES), F32),
+            jax.ShapeDtypeStruct((tokens, rank), F32),
+            jax.ShapeDtypeStruct((tokens // 2, 2 * rope_width), F32),
         ),
         in_specs=[
             whole(latent_in), whole(raw_key), whole(gain), whole(cos), whole(sin),
@@ -281,16 +311,17 @@
         out_specs=(
             cut(tokens, 2 * width),
             cut(tokens, 2 * rope_width),
-            pl.BlockSpec((tokens, LANES), lambda i: (0, 0)),
+            pl.BlockSpec((tokens, rank), lambda i: (0, 0)),
+            pl.BlockSpec((tokens // 2, 2 * rope_width), lambda i: (0, 0)),
         ),
         scratch_shapes=[
             pltpu.VMEM((tokens, rank), BF16),
-            pltpu.VMEM((tokens, rope_width), BF16),
+            pltpu.VMEM((rope_width, tokens), BF16),
             pltpu.VMEM((tokens, rank), F32),
             pltpu.VMEM((tokens, rope_width), F32),
         ],
         name="attention_back",
-    )(latent_in, raw_key, gain, cos, sin, query, rope, cot, key_full, value_full)
+    )(latent_in, raw_key, gain, jnp.asarray(cos), jnp.asarray(sin), query, rope, cot, key_full, value_full)
 
 
 def tail_tables(rows_out):
@@ -313,9 +344,9 @@
 
 
 def tail_kernel(
-    part_ref, latent_ref, gain_ref, cos_ref, sin_ref, hidden_ref, order_ref, rows_ref, out_ref,
-    sum_recv, kv_own, quad_out, quad_in, block_out, block_all, y_out, y_in,
-    s1, r1, s2, r2, s3, r3, s4, r4,
+    part_ref, rope_part_ref, latent_ref, gain_ref, cos_ref, sin_ref, hidden_ref, order_ref,
+    rows_ref, out_ref, sum_recv, rope_recv, kv_own, quad_out, quad_in, block_out, block_all, y_out, y_in,
+    s1, r1, s2, r2, s3, r3, s4, r4, s5, r5,
 ):
     dp = lax.axis_index("dp")
     head = lax.axis_index("head")
@@ -377,28 +408,43 @@
             device_id_type=MESH,
         )
 
+    def rope_copy(k):
+        return pltpu.make_async_remote_copy(
+            src_ref=rope_part_ref.at[rows_of(head_peer(k), CHUNK // 2)],
+            dst_ref=rope_recv.at[k],
+            send_sem=s5.at[k],
+            recv_sem=r5.at[k],
+            device_id={"head": head_peer(k)},
+            device_id_type=MESH,
+        )
+
     @pl.loop(1, HEAD_RANKS)
     def _(k):
         sum_copy(k).start()
+        rope_copy(k).start()
 
     mine = rows_of(head, CHUNK)
     x = latent_ref[mine, :].astype(F32)
     inv = lax.rsqrt(jnp.mean(x * x, axis=1, keepdims=True) + norm_eps)
     cos, sin = cos_ref[mine, :], sin_ref[mine, :]
     total = part_ref[mine, :]
+    rope_sum = rope_part_ref[rows_of(head, CHUNK // 2), :]
     iota = lax.broadcasted_iota(jnp.int32, (LANES, LANES), 0)
     select = jnp.where(iota == order_ref[...], 1.0, 0.0).astype(BF16)
 
     @pl.loop(1, HEAD_RANKS)
     def _(k):
         sum_copy(k).wait()
+        rope_copy(k).wait()
 
     for k in range(1, HEAD_RANKS):
         total += sum_recv[k]
-    scaled = gain_ref[...] * total[:, :rank]
+        rope_sum += rope_recv[k]
+    scaled = gain_ref[...] * total
     inner = jnp.sum(x * scaled, axis=1, keepdims=True)
     latent_grad = inv * scaled - x * (inv * inv * inv) * inner / rank
-    g, q = total[:, rank : rank + half], total[:, rank + half : rank + rope_width]
+    rope_sum = jnp.concatenate((rope_sum[:, :rope_width], rope_sum[:, rope_width:]), axis=0)
+    g, q = rope_sum[:, :half], rope_sum[:, half:]
     rope_grad = jnp.concatenate(
         (
             g * cos + q * sin,
@@ -467,17 +513,28 @@
     def _(k):
         block_copy(k).wait()
 
-    grad = jnp.zeros((Y_SIZE * SLOT, hidden_ref.shape[1]), F32)
+    cols = out_ref.shape[1]
+    grad = jnp.zeros((Y_SIZE * SLOT, cols), F32)
     for m in range(QUAD):
         picked = dot(pick, block_all[m], NT) + dot(pick_rest[m], block_all[QUAD], NT)
         grad += dot(
-            picked.astype(BF16), hidden_ref[m * tokens : (m + 1) * tokens, :], NN
-        )
-    y_out[...] = grad
+            picked.astype(BF16), hidden_ref[m * cols : (m + 1) * cols, :], NT
+        )
+    full = cols // 128
+    rest_rows = rows_out // 2
+    y_out[...] = jnp.zeros_like(y_out)
+    for y in range(Y_SIZE):
+        piece = grad[y * SLOT : y * SLOT + rows_out]
+        for t in range(full):
+            y_out[y, t * rows_out : (t + 1) * rows_out, :] = piece[:, t * 128 : (t + 1) * 128]
+        edge = piece[:, full * 128 :]
+        y_out[y, full * rows_out : full * rows_out + rest_rows, :] = jnp.concatenate(
+            (edge[:rest_rows], edge[rest_rows:]), axis=1
+        )
 
     def y_copy(k):
         return pltpu.make_async_remote_copy(
-            src_ref=y_out.at[rows_of(y_peer(k), SLOT)],
+            src_ref=y_out.at[y_peer(k)],
             dst_ref=y_in.at[k],
             send_sem=s4.at[k],
             recv_sem=r4.at[k],
@@ -489,7 +546,7 @@
     def _(k):
         y_copy(k).start()
 
-    first = y_out[rows_of(y_pos, SLOT), :]
+    first = y_out[y_pos]
 
     @pl.loop(1, Y_SIZE)
     def _(k):
@@ -497,34 +554,40 @@
 
     for k in range(1, Y_SIZE):
         first += y_in[k]
-    out_ref[...] = first[:rows_out, :]
-
-
-def tail(part, latent_in, gain, cos, sin, hidden_quad, rows_out):
+    for t in range(full):
+        out_ref[:, t * 128 : (t + 1) * 128] = first[t * rows_out : (t + 1) * rows_out]
+    edge = first[full * rows_out : full * rows_out + rest_rows]
+    out_ref[:rest_rows, full * 128 :] = edge[:, :64]
+    out_ref[rest_rows:, full * 128 :] = edge[:, 64:]
+
+
+def tail(part, rope_part, latent_in, gain, cos, sin, hidden_quad, rows_out):
     tokens = latent_in.shape[0]
-    cols = hidden_quad.shape[1]
+    cols = hidden_quad.shape[0] // QUAD
     dma = pltpu.SemaphoreType.DMA
     order, rows = tail_tables(rows_out)
     return pl.pallas_call(
         tail_kernel,
         out_shape=jax.ShapeDtypeStruct((rows_out, cols), F32),
-        in_specs=[VMEM_SPEC] * 8,
+        in_specs=[VMEM_SPEC] * 9,
         out_specs=VMEM_SPEC,
         scratch_shapes=[
-            pltpu.VMEM((HEAD_RANKS, CHUNK, LANES), F32),
+            pltpu.VMEM((HEAD_RANKS, CHUNK, latent_in.shape[1]), F32),
+            pltpu.VMEM((HEAD_RANKS, CHUNK // 2, 128), F32),
             pltpu.VMEM((CHUNK, LANES), BF16),
             pltpu.VMEM((QUAD, 2, CHUNK, 128), BF16),
             pltpu.VMEM((QUAD, 2, CHUNK, 128), BF16),
             pltpu.VMEM((QUAD + 1, CHUNK, 128), BF16),
             pltpu.VMEM((QUAD + 1, tokens, 128), BF16),
-            pltpu.VMEM((Y_SIZE * SLOT, cols), F32),
-            pltpu.VMEM((Y_SIZE, SLOT, cols), F32),
+            pltpu.VMEM((Y_SIZE, PACKED, 128), F32),
+            pltpu.VMEM((Y_SIZE, PACKED, 128), F32),
             dma((HEAD_RANKS,)), dma((HEAD_RANKS,)), dma((QUAD,)), dma((QUAD,)),
             dma((HEAD_RANKS,)), dma((HEAD_RANKS,)), dma((Y_SIZE,)), dma((Y_SIZE,)),
+            dma((HEAD_RANKS,)), dma((HEAD_RANKS,)),
         ],
         compiler_params=pltpu.CompilerParams(collective_id=1, has_side_effects=True),
         name="tail",
-    )(part, latent_in, gain, cos, sin, hidden_quad, jnp.asarray(order), jnp.asarray(rows))
+    )(part, rope_part, latent_in, gain, jnp.asarray(cos), jnp.asarray(sin), hidden_quad, jnp.asarray(order), jnp.asarray(rows))
 
 
 def local(
@@ -544,17 +607,16 @@
     row_count = latent_unnormed.shape[0]
     dp_size = lax.axis_size("dp")
     cos, sin = angle_tables(unrotated_key.shape[1])
-    cos, sin = jnp.asarray(cos), jnp.asarray(sin)
     gain = latent_norm_scale[None, :]
     key_full, value_full, hidden_quad = gather_up(
-        key_up_matrix, value_up_matrix, hidden_in, dp_size
-    )
-    grad_query, grad_rope, part = attention_back(
-        latent_unnormed, unrotated_key, gain, cos, sin,
+        key_up_matrix, value_up_matrix, hidden_in.T, dp_size
+    )
+    grad_query, grad_rope, part, rope_part = attention_back(
+        latent_unnormed, unrotated_key.T, gain, cos.T, sin.T,
         plain_query_rows, rotated_query_rows, output_cotangent, key_full, value_full,
     )
     weight_sum = tail(
-        part, latent_unnormed, gain, cos, sin, hidden_quad, down_weight.shape[0]
+        part, rope_part, latent_unnormed, gain, cos, sin, hidden_quad, down_weight.shape[0]
     )
     weight_grad = weight_sum / (row_count * dp_size)
     new_first = beta_one * first_moment + (1.0 - beta_one) * weight_grad

time: 102 us -> 96.4 us (0.945)
  local copies, waits for them, and re-layouts: 3.29 us -> 0.02 us
  Pallas kernels: 94.7 us -> 92.4 us
    unnamed x8 -> x6, local copies, waits for them, and re-layouts: 3.29 us -> 0.02 us
    pallas_call x1, Pallas kernels: 54.8 us -> 51.6 us  [tail(): pl.pallas_call(tail_kernel, out_shape=jax.ShapeDtypeStruct((rows_out, col...]
    pallas_call x1, Pallas kernels: 29.2 us -> 30.3 us  [gather_up(): pl.pallas_call(gather_kernel, out_shape=(full, full, jax.ShapeDtypeStruct...]
where the time goes in v3:
time: 96.4 us; the launch traced here: 94.6 us
  Pallas kernels  92.4 us (96%)
  other arithmetic  1.47 us (2%)
    pallas_call x1, Pallas kernels, tail(): pl.pallas_call(tail_kernel, out_shape=jax.ShapeDtypeStruct((rows_out, col...  51.6 us
    pallas_call x1, Pallas kernels, gather_up(): pl.pallas_call(gather_kernel, out_shape=(full, full, jax.ShapeDtypeStruct...  30.3 us
    pallas_call x1, Pallas kernels, attention_back(): pl.pallas_call(functools.partial(attention_kernel, scale_factor), grid=(h...  10.5 us

profile of v3, /device:TPU:1, one launch (start us, length us, event | category | flops | bytes accessed | tf_op | source)
XLA Modules:
  0.0 94.6 jit_solution(7605084882569646343)
XLA Ops:
  0.6 30.3 %gather_up.1 = (bf16[512,1024]{1,0:T(8,128)(2,1)}, bf16[512,1024]{1,0:T(8,128)(2,1)}, bf16[1792,256]{1,0:T(8,128)(2,1)}) custom-call(bf16[16,1024]{1,0:T(8,128)(2,1)} %key_ref.1, bf16[16,1024]{1,0:T(8,128)(2,1)} %value_ref.1, bf16[448,256]{1,0:T(8,128)(2,1)} %bitcast.3), custom_call_target="tpu_custom_call" | custom-call | tf_op jit(solution)/shard_map/gather_up/pallas_call | solution.py:197
  31.0 10.5 %attention_back.1 = (bf16[256,1024]{1,0:T(8,128)(2,1)}, bf16[256,512]{1,0:T(8,128)(2,1)}, f32[256,512]{1,0:T(8,128)}, f32[128,128]{1,0:T(8,128)}) custom-call(bf16[256,512]{1,0:T(8,128)(2,1)} %latent_ref.3, bf16[64,256]{1,0:T(8,128)(2,1)} %bitcast.4, f32[1,512]{1,0:T(1,128)} %bitcast.5, f32[32,256]{1,0:T(8,128)} %constant.36.clone.cos_ref, ...), custom_call_target="tpu_custom_call" | custom-call | tf_op jit(solution)/shard_map/attention_back/pallas_call | solution.py:297
  41.4 0.0 copy-start
  41.5 0.0 copy-start.1
  41.5 0.0 copy-start.2
  41.5 51.6 %tail.1 = f32[18,448]{1,0:T(8,128)} custom-call(f32[256,512]{1,0:T(8,128)} %get-tuple-element.16.part_ref, f32[128,128]{1,0:T(8,128)} %get-tuple-element.17.rope_part_ref, bf16[256,512]{1,0:T(8,128)(2,1)} %latent_ref.3, f32[1,512]{1,0:T(1,128)} %bitcast.6, f32[256,32]{1,0:T(8,128)} %constant.38.clone.cos_ref, f32[256,32]{1,0:T(8,128)} %constant.39.clone.sin_ref, ...), custom_call_target="tpu_custom_call" | custom-call | tf_op jit(solution)/shard_map/tail/pallas_call | solution.py:569
  93.1 0.0 copy-done
  93.1 0.0 copy-done.1
  93.1 0.0 copy-done.2
  93.1 1.5 %multiply_subtract_fusion = (f32[18,448]{1,0:T(8,128)}, f32[18,448]{1,0:T(8,128)}, f32[18,448]{1,0:T(8,128)}) fusion(f32[18,448]{1,0:T(8,128)S(1)} %copy-done, f32[18,448]{1,0:T(8,128)} %tail.1, f32[18,448]{1,0:T(8,128)S(1)} %copy-done.1, f32[18,448]{1,0:T(8,128)S(1)} %copy-done.2), kind=kLoop, calls=%fused_computation | loop fusion | flops 129024 | bytes 225792 | tf_op jit(solution)/shard_map/sub | solution.py:625
Async XLA Ops:
  41.4 51.7 %copy-start = (f32[18,448]{1,0:T(8,128)S(1)}, f32[18,448]{1,0:T(8,128)}, u32[]{:S(2)}) copy-start(f32[18,448]{1,0:T(8,128)} %param.27) | copy-start | bytes 96772
  41.5 51.7 %copy-start.1 = (f32[18,448]{1,0:T(8,128)S(1)}, f32[18,448]{1,0:T(8,128)}, u32[]{:S(2)}) copy-start(f32[18,448]{1,0:T(8,128)} %param.28) | copy-start | bytes 96772
  41.5 51.7 %copy-start.2 = (f32[18,448]{1,0:T(8,128)S(1)}, f32[18,448]{1,0:T(8,128)}, u32[]{:S(2)}) copy-start(f32[18,448]{1,0:T(8,128)} %param.29) | copy-start | bytes 96772

commit v4 on v3

--- a/solution.py
+++ b/solution.py
@@ -239,7 +239,8 @@
         raw = raw_ref[...].astype(F32)
         u, w = raw[:half], raw[half:]
         cos, sin = cos_ref[...], sin_ref[...]
-        key_rot[...] = jnp.concatenate((u * cos - w * sin, u * sin + w * cos), axis=0).astype(BF16)
+        rotated = jnp.concatenate((u * cos - w * sin, u * sin + w * cos), axis=0)
+        key_rot[...] = rotated.T.astype(BF16)
         total[...] = jnp.zeros_like(total)
         rope_total[...] = jnp.zeros_like(rope_total)
 
@@ -248,7 +249,7 @@
     keys2 = dot(latent[...], key_up_ref[...], NN).astype(BF16)
     values2 = dot(latent[...], value_up_ref[...], NN).astype(BF16)
     rot = key_rot[...]
-    causal = lax.broadcasted_iota(jnp.int32, (tokens, tokens), 0) >= lax.broadcasted_iota(
+    causal = lax.broadcasted_iota(jnp.int32, (tokens, tokens), 0) <= lax.broadcasted_iota(
         jnp.int32, (tokens, tokens), 1
     )
     grad_keys, grad_values, grad_ropes = [], [], []
@@ -259,19 +260,19 @@
         cot = cot_ref[:, cols]
         key = keys2[:, cols]
         value = values2[:, cols]
-        scores = (dot(query, key, NT) + dot(rope, rot, NN)) * scale_factor
+        scores = (dot(key, query, NT) + dot(rot, rope, NT)) * scale_factor
         scores = jnp.where(causal, scores, -1e30)
-        grown = jnp.exp(scores - jnp.max(scores, axis=1, keepdims=True))
-        probs = grown / jnp.sum(grown, axis=1, keepdims=True)
+        grown = jnp.exp(scores - jnp.max(scores, axis=0, keepdims=True))
+        probs = grown * (1.0 / jnp.sum(grown, axis=0, keepdims=True))
         prob_low = probs.astype(BF16)
-        grad_probs = dot(cot, value, NT)
-        delta = jnp.sum(prob_low.astype(F32) * grad_probs, axis=1, keepdims=True)
+        grad_probs = dot(value, cot, NT)
+        delta = jnp.sum(prob_low.astype(F32) * grad_probs, axis=0, keepdims=True)
         score_low = (probs * (grad_probs - delta) * scale_factor).astype(BF16)
-        grad_query_ref[:, cols] = dot(score_low, key, NN).astype(BF16)
-        grad_ropes.append(dot(score_low, rot, NT).astype(BF16))
-        grad_keys.append(dot(score_low, query, TN).astype(BF16))
-        grad_values.append(dot(prob_low, cot, TN).astype(BF16))
-        rope_total[...] += dot(score_low, rope, TN)
+        grad_query_ref[:, cols] = dot(score_low, key, TN).astype(BF16)
+        grad_ropes.append(dot(score_low, rot, TN).astype(BF16))
+        grad_keys.append(dot(score_low, query, NN).astype(BF16))
+        grad_values.append(dot(prob_low, cot, NN).astype(BF16))
+        rope_total[...] += dot(score_low, rope, NN)
     grad_rope_ref[...] = jnp.concatenate(grad_ropes, axis=1)
     total[...] += dot(jnp.concatenate(grad_keys, axis=1), key_up_ref[...], NT) + dot(
         jnp.concatenate(grad_values, axis=1), value_up_ref[...], NT
@@ -316,7 +317,7 @@
         ),
         scratch_shapes=[
             pltpu.VMEM((tokens, rank), BF16),
-            pltpu.VMEM((rope_width, tokens), BF16),
+            pltpu.VMEM((tokens, rope_width), BF16),
             pltpu.VMEM((tokens, rank), F32),
             pltpu.VMEM((tokens, rope_width), F32),
         ],
@@ -341,6 +342,10 @@
     for y in range(Y_SIZE):
         rows[y * SLOT : y * SLOT + rows_out, 0] = y * rows_out + np.arange(rows_out)
     return order, rows
+
+
+def far_first(i, size):
+    return size // 2 + (1 - 2 * lax.rem(i, 2)) * ((i + 1) // 2)
 
 
 def tail_kernel(
@@ -418,8 +423,9 @@
             device_id_type=MESH,
         )
 
-    @pl.loop(1, HEAD_RANKS)
-    def _(k):
+    @pl.loop(0, HEAD_RANKS - 1)
+    def _(i):
+        k = far_first(i, HEAD_RANKS)
         sum_copy(k).start()
         rope_copy(k).start()
 
@@ -496,9 +502,9 @@
             device_id_type=MESH,
         )
 
-    @pl.loop(1, HEAD_RANKS)
-    def _(k):
-        block_copy(k).start()
+    @pl.loop(0, HEAD_RANKS - 1)
+    def _(i):
+        block_copy(far_first(i, HEAD_RANKS)).start()
 
     block_all[:, mine, :] = block_out[...]
     q_row = rows_ref[...]
@@ -542,9 +548,9 @@
             device_id_type=MESH,
         )
 
-    @pl.loop(1, Y_SIZE)
-    def _(k):
-        y_copy(k).start()
+    @pl.loop(0, Y_SIZE - 1)
+    def _(i):
+        y_copy(far_first(i, Y_SIZE)).start()
 
     first = y_out[y_pos]
 

time: 96.4 us -> 94.3 us (0.978); the launches traced: 94.6 us -> 94 us
    pallas_call x1, Pallas kernels: 10.5 us -> 9.27 us  [attention_back(): pl.pallas_call(functools.partial(attention_kernel, scale_factor), grid=(h...]
where the time goes in v4:
time: 94.3 us; the launch traced here: 94 us
  Pallas kernels  91.8 us (97%)
  other arithmetic  1.47 us (2%)
    pallas_call x1, Pallas kernels, tail(): pl.pallas_call(tail_kernel, out_shape=jax.ShapeDtypeStruct((rows_out, col...  52.2 us
    pallas_call x1, Pallas kernels, gather_up(): pl.pallas_call(gather_kernel, out_shape=(full, full, jax.ShapeDtypeStruct...  30.3 us
    pallas_call x1, Pallas kernels, attention_back(): pl.pallas_call(functools.partial(attention_kernel, scale_factor), grid=(h...  9.27 us

profile of v4, /device:TPU:1, one launch (start us, length us, event | category | flops | bytes accessed | tf_op | source)
XLA Modules:
  0.0 94.0 jit_solution(11606549061953595292)
XLA Ops:
  0.6 30.3 %gather_up.1 = (bf16[512,1024]{1,0:T(8,128)(2,1)}, bf16[512,1024]{1,0:T(8,128)(2,1)}, bf16[1792,256]{1,0:T(8,128)(2,1)}) custom-call(bf16[16,1024]{1,0:T(8,128)(2,1)} %key_ref.1, bf16[16,1024]{1,0:T(8,128)(2,1)} %value_ref.1, bf16[448,256]{1,0:T(8,128)(2,1)} %bitcast.3), custom_call_target="tpu_custom_call" | custom-call | tf_op jit(solution)/shard_map/gather_up/pallas_call | solution.py:197
  31.0 9.3 %attention_back.1 = (bf16[256,1024]{1,0:T(8,128)(2,1)}, bf16[256,512]{1,0:T(8,128)(2,1)}, f32[256,512]{1,0:T(8,128)}, f32[128,128]{1,0:T(8,128)}) custom-call(bf16[256,512]{1,0:T(8,128)(2,1)} %latent_ref.3, bf16[64,256]{1,0:T(8,128)(2,1)} %bitcast.4, f32[1,512]{1,0:T(1,128)} %bitcast.5, f32[32,256]{1,0:T(8,128)} %constant.36.clone.cos_ref, ...), custom_call_target="tpu_custom_call" | custom-call | tf_op jit(solution)/shard_map/attention_back/pallas_call | solution.py:298
  40.3 0.0 copy-start
  40.3 0.0 copy-start.1
  40.3 0.0 copy-start.2
  40.3 52.2 %tail.1 = f32[18,448]{1,0:T(8,128)} custom-call(f32[256,512]{1,0:T(8,128)} %get-tuple-element.16.part_ref, f32[128,128]{1,0:T(8,128)} %get-tuple-element.17.rope_part_ref, bf16[256,512]{1,0:T(8,128)(2,1)} %latent_ref.3, f32[1,512]{1,0:T(1,128)} %bitcast.6, f32[256,32]{1,0:T(8,128)} %constant.38.clone.cos_ref, f32[256,32]{1,0:T(8,128)} %constant.39.clone.sin_ref, ...), custom_call_target="tpu_custom_call" | custom-call | tf_op jit(solution)/shard_map/tail/pallas_call | solution.py:575
  92.5 0.0 copy-done
  92.5 0.0 copy-done.1
  92.5 0.0 copy-done.2
  92.5 1.5 %multiply_subtract_fusion = (f32[18,448]{1,0:T(8,128)}, f32[18,448]{1,0:T(8,128)}, f32[18,448]{1,0:T(8,128)}) fusion(f32[18,448]{1,0:T(8,128)S(1)} %copy-done, f32[18,448]{1,0:T(8,128)} %tail.1, f32[18,448]{1,0:T(8,128)S(1)} %copy-done.1, f32[18,448]{1,0:T(8,128)S(1)} %copy-done.2), kind=kLoop, calls=%fused_computation | loop fusion | flops 129024 | bytes 225792 | tf_op jit(solution)/shard_map/sub | solution.py:631
Async XLA Ops:
  40.3 52.3 %copy-start = (f32[18,448]{1,0:T(8,128)S(1)}, f32[18,448]{1,0:T(8,128)}, u32[]{:S(2)}) copy-start(f32[18,448]{1,0:T(8,128)} %param.27) | copy-start | bytes 96772
  40.3 52.3 %copy-start.1 = (f32[18,448]{1,0:T(8,128)S(1)}, f32[18,448]{1,0:T(8,128)}, u32[]{:S(2)}) copy-start(f32[18,448]{1,0:T(8,128)} %param.28) | copy-start | bytes 96772
  40.3 52.3 %copy-start.2 = (f32[18,448]{1,0:T(8,128)S(1)}, f32[18,448]{1,0:T(8,128)}, u32[]{:S(2)}) copy-start(f32[18,448]{1,0:T(8,128)} %param.29) | copy-start | bytes 96772

commit v5 on v4

--- a/solution.py
+++ b/solution.py
@@ -44,7 +44,7 @@
     return np.cos(angles).astype(np.float32), np.sin(angles).astype(np.float32)
 
 
-def gather_kernel(
+def gather_body(
     key_ref, value_ref, hidden_ref, key_out, value_out, hidden_out,
     y_send, y_recv, x_send, x_recv, c_send, c_recv, own_sem, h_send, h_recv,
 ):
@@ -61,11 +61,6 @@
     ups = (place(x_pos, y_pos + 1, core), place(x_pos, y_pos - 1, core))
     x_partner = place(other_x, y_pos, core)
     c_partner = place(x_pos, y_pos, 1 - core)
-
-    barrier = pltpu.get_barrier_semaphore()
-    for peer in (ups[0], ups[1], x_partner, c_partner):
-        pl.semaphore_signal(barrier, inc=1, device_id={"dp": peer}, device_id_type=MESH)
-    pl.semaphore_wait(barrier, 4)
 
     rows_in = key_ref.shape[0]
     sources = (key_ref, value_ref)
@@ -179,35 +174,18 @@
     hidden_d = send_hidden(far, far, 2, c_partner)
     for copy in own:
         copy.wait()
-    for copy in x_copies.values():
-        copy.wait_send()
-    for copy in y_copies.values():
-        copy.wait_send()
     for copy in c_copies.values():
-        copy.wait()
-    hidden_x.wait_send()
-    hidden_c.wait()
-    hidden_d.wait()
-
-
-def gather_up(key_up, value_up, hidden, dp_size):
-    rows, cols = key_up.shape
-    full = jax.ShapeDtypeStruct((rows * dp_size, cols), key_up.dtype)
-    dma = pltpu.SemaphoreType.DMA
-    return pl.pallas_call(
-        gather_kernel,
-        out_shape=(
-            full, full, jax.ShapeDtypeStruct((QUAD * hidden.shape[0], hidden.shape[1]), BF16)
-        ),
-        in_specs=[VMEM_SPEC] * 3,
-        out_specs=(VMEM_SPEC,) * 3,
-        scratch_shapes=[
-            dma((21,)), dma((21,)), dma((9,)), dma((9,)), dma((32,)), dma((32,)), dma((3,)),
-            dma((3,)), dma((3,)),
-        ],
-        compiler_params=pltpu.CompilerParams(collective_id=0, has_side_effects=True),
-        name="gather_up",
-    )(key_up, value_up, hidden)
+        copy.wait_recv()
+
+    def finish():
+        for group in (x_copies, y_copies, c_copies):
+            for copy in group.values():
+                copy.wait_send()
+        hidden_x.wait_send()
+        hidden_c.wait()
+        hidden_d.wait()
+
+    return finish
 
 
 def dot(a, b, dims):
@@ -219,45 +197,47 @@
 TN = ((0,), (0,))
 
 
-def attention_kernel(
-    scale_factor,
-    latent_ref, raw_ref, gain_ref, cos_ref, sin_ref,
-    query_ref, rope_ref, cot_ref, key_up_ref, value_up_ref,
-    grad_query_ref, grad_rope_ref, part_ref, rope_part_ref,
+def attention_start(latent_ref, raw_ref, gain_ref, cos_ref, sin_ref, latent, key_rot, total, rope_total):
+    half = raw_ref.shape[0] // 2
+    x = latent_ref[...].astype(F32)
+    inv = lax.rsqrt(jnp.mean(x * x, axis=1, keepdims=True) + norm_eps)
+    latent[...] = (x * inv * gain_ref[...]).astype(BF16)
+    raw = raw_ref[...].astype(F32)
+    u, w = raw[:half], raw[half:]
+    cos, sin = cos_ref[...], sin_ref[...]
+    rotated = jnp.concatenate((u * cos - w * sin, u * sin + w * cos), axis=0)
+    key_rot[...] = rotated.T.astype(BF16)
+    total[...] = jnp.zeros_like(total)
+    rope_total[...] = jnp.zeros_like(rope_total)
+
+
+def attention_pair(
+    scale_factor, width, pair,
+    query_ref, rope_ref, cot_ref, key_up_ref, value_up_ref, grad_query_ref, grad_rope_ref,
     latent, key_rot, total, rope_total,
 ):
-    step = pl.program_id(0)
-    rank = latent_ref.shape[1]
-    rope_width = raw_ref.shape[0]
-    half = rope_width // 2
-
-    @pl.when(step == 0)
-    def _():
-        x = latent_ref[...].astype(F32)
-        inv = lax.rsqrt(jnp.mean(x * x, axis=1, keepdims=True) + norm_eps)
-        latent[...] = (x * inv * gain_ref[...]).astype(BF16)
-        raw = raw_ref[...].astype(F32)
-        u, w = raw[:half], raw[half:]
-        cos, sin = cos_ref[...], sin_ref[...]
-        rotated = jnp.concatenate((u * cos - w * sin, u * sin + w * cos), axis=0)
-        key_rot[...] = rotated.T.astype(BF16)
-        total[...] = jnp.zeros_like(total)
-        rope_total[...] = jnp.zeros_like(rope_total)
-
-    tokens = latent_ref.shape[0]
-    width = query_ref.shape[1] // 2
-    keys2 = dot(latent[...], key_up_ref[...], NN).astype(BF16)
-    values2 = dot(latent[...], value_up_ref[...], NN).astype(BF16)
+    tokens = latent.shape[0]
+    rope_width = key_rot.shape[1]
+
+    def columns(size):
+        return pl.ds(pl.multiple_of(pair * size, size), size)
+
+    both = columns(2 * width)
+    key_up, value_up = key_up_ref[:, both], value_up_ref[:, both]
+    queries, cots = query_ref[:, both], cot_ref[:, both]
+    ropes = rope_ref[:, columns(2 * rope_width)]
+    keys2 = dot(latent[...], key_up, NN).astype(BF16)
+    values2 = dot(latent[...], value_up, NN).astype(BF16)
     rot = key_rot[...]
     causal = lax.broadcasted_iota(jnp.int32, (tokens, tokens), 0) <= lax.broadcasted_iota(
         jnp.int32, (tokens, tokens), 1
     )
-    grad_keys, grad_values, grad_ropes = [], [], []
+    grad_queries, grad_keys, grad_values, grad_ropes = [], [], [], []
     for h in range(2):
         cols = slice(h * width, (h + 1) * width)
-        query = query_ref[:, cols]
-        rope = rope_ref[:, h * rope_width : (h + 1) * rope_width]
-        cot = cot_ref[:, cols]
+        query = queries[:, cols]
+        rope = ropes[:, h * rope_width : (h + 1) * rope_width]
+        cot = cots[:, cols]
         key = keys2[:, cols]
         value = values2[:, cols]
         scores = (dot(key, query, NT) + dot(rot, rope, NT)) * scale_factor
@@ -268,61 +248,16 @@
         grad_probs = dot(value, cot, NT)
         delta = jnp.sum(prob_low.astype(F32) * grad_probs, axis=0, keepdims=True)
         score_low = (probs * (grad_probs - delta) * scale_factor).astype(BF16)
-        grad_query_ref[:, cols] = dot(score_low, key, TN).astype(BF16)
+        grad_queries.append(dot(score_low, key, TN).astype(BF16))
         grad_ropes.append(dot(score_low, rot, TN).astype(BF16))
         grad_keys.append(dot(score_low, query, NN).astype(BF16))
         grad_values.append(dot(prob_low, cot, NN).astype(BF16))
         rope_total[...] += dot(score_low, rope, NN)
-    grad_rope_ref[...] = jnp.concatenate(grad_ropes, axis=1)
-    total[...] += dot(jnp.concatenate(grad_keys, axis=1), key_up_ref[...], NT) + dot(
-        jnp.concatenate(grad_values, axis=1), value_up_ref[...], NT
-    )
-
-    @pl.when(step == pl.num_programs(0) - 1)
-    def _():
-        part_ref[...] = total[...]
-        pairs = rope_total[...].reshape(tokens // CHUNK, 2, CHUNK // 2, rope_width)
-        rope_part_ref[...] = jnp.concatenate((pairs[:, 0], pairs[:, 1]), axis=2).reshape(
-            tokens // 2, 2 * rope_width
-        )
-
-
-def attention_back(latent_in, raw_key, gain, cos, sin, query, rope, cot, key_full, value_full):
-    tokens, rank = latent_in.shape
-    rope_width = raw_key.shape[0]
-    heads = rope.shape[1] // rope_width
-    width = query.shape[1] // heads
-    whole = lambda a: pl.BlockSpec(a.shape, lambda i: (0, 0))
-    cut = lambda rows, cols: pl.BlockSpec((rows, cols), lambda i: (0, i))
-    scale_factor = 1.0 / math.sqrt(width + rope_width)
-    return pl.pallas_call(
-        functools.partial(attention_kernel, scale_factor),
-        grid=(heads // 2,),
-        out_shape=(
-            jax.ShapeDtypeStruct(query.shape, BF16),
-            jax.ShapeDtypeStruct(rope.shape, BF16),
-            jax.ShapeDtypeStruct((tokens, rank), F32),
-            jax.ShapeDtypeStruct((tokens // 2, 2 * rope_width), F32),
-        ),
-        in_specs=[
-            whole(latent_in), whole(raw_key), whole(gain), whole(cos), whole(sin),
-            cut(tokens, 2 * width), cut(tokens, 2 * rope_width), cut(tokens, 2 * width),
-            cut(rank, 2 * width), cut(rank, 2 * width),
-        ],
-        out_specs=(
-            cut(tokens, 2 * width),
-            cut(tokens, 2 * rope_width),
-            pl.BlockSpec((tokens, rank), lambda i: (0, 0)),
-            pl.BlockSpec((tokens // 2, 2 * rope_width), lambda i: (0, 0)),
-        ),
-        scratch_shapes=[
-            pltpu.VMEM((tokens, rank), BF16),
-            pltpu.VMEM((tokens, rope_width), BF16),
-            pltpu.VMEM((tokens, rank), F32),
-            pltpu.VMEM((tokens, rope_width), F32),
-        ],
-        name="attention_back",
-    )(latent_in, raw_key, gain, jnp.asarray(cos), jnp.asarray(sin), query, rope, cot, key_full, value_full)
+    grad_query_ref[:, both] = jnp.concatenate(grad_queries, axis=1)
+    grad_rope_ref[:, columns(2 * rope_width)] = jnp.concatenate(grad_ropes, axis=1)
+    total[...] += dot(jnp.concatenate(grad_keys, axis=1), key_up, NT) + dot(
+        jnp.concatenate(grad_values, axis=1), value_up, NT
+    )
 
 
 def tail_tables(rows_out):
@@ -348,8 +283,8 @@
     return size // 2 + (1 - 2 * lax.rem(i, 2)) * ((i + 1) // 2)
 
 
-def tail_kernel(
-    part_ref, rope_part_ref, latent_ref, gain_ref, cos_ref, sin_ref, hidden_ref, order_ref,
+def tail_body(
+    attention, part_ref, rope_part_ref, latent_ref, gain_ref, cos_ref, sin_ref, hidden_ref, order_ref,
     rows_ref, out_ref, sum_recv, rope_recv, kv_own, quad_out, quad_in, block_out, block_all, y_out, y_in,
     s1, r1, s2, r2, s3, r3, s4, r4, s5, r5,
 ):
@@ -398,7 +333,7 @@
     def _(k):
         pl.semaphore_signal(barrier, inc=1, device_id={"dp": quad_device(k)}, device_id_type=MESH)
 
-    pl.semaphore_wait(barrier, HEAD_RANKS - 1 + Y_SIZE - 1 + QUAD - 1)
+    attention(lambda: pl.semaphore_wait(barrier, HEAD_RANKS - 1 + Y_SIZE - 1 + QUAD - 1))
 
     def rows_of(index, size):
         return pl.ds(pl.multiple_of(index * size, size), size)
@@ -567,18 +502,100 @@
     out_ref[rest_rows:, full * 128 :] = edge[:, 64:]
 
 
-def tail(part, rope_part, latent_in, gain, cos, sin, hidden_quad, rows_out):
-    tokens = latent_in.shape[0]
-    cols = hidden_quad.shape[0] // QUAD
+def fused_kernel(scale_factor, width, count, *refs):
+    refs = list(refs)
+
+    def take(n):
+        taken = refs[:n]
+        del refs[:n]
+        return taken
+
+    key_in, value_in, hidden_in, latent_ref, raw_ref, gain_ref = take(6)
+    cos_t, sin_t, cos_ref, sin_ref, order_ref, rows_ref = take(6)
+    loads = take(3)
+    grad_query_ref, grad_rope_ref, out_ref = take(3)
+    key_full, value_full, hidden_quad = take(3)
+    latent, key_rot, total, rope_total, rope_part = take(5)
+    buffers = take(3)
+    load_sem = take(1)[0]
+    gather_sems = take(9)
+
+    copies = [
+        pltpu.make_async_copy(loads[n], buffers[n], load_sem.at[n]) for n in range(3)
+    ]
+
+    def attention(enter):
+        for copy in copies:
+            copy.start()
+        attention_start(
+            latent_ref, raw_ref, gain_ref, cos_t, sin_t, latent, key_rot, total, rope_total
+        )
+        enter()
+        finish = gather_body(
+            key_in, value_in, hidden_in, key_full, value_full, hidden_quad, *gather_sems
+        )
+        for copy in copies:
+            copy.wait()
+
+        @pl.loop(0, count)
+        def _(pair):
+            attention_pair(
+                scale_factor, width, pair, *buffers, key_full, value_full,
+                grad_query_ref, grad_rope_ref, latent, key_rot, total, rope_total,
+            )
+
+        finish()
+        tokens, rope_width = rope_total.shape
+        pairs = rope_total[...].reshape(tokens // CHUNK, 2, CHUNK // 2, rope_width)
+        rope_part[...] = jnp.concatenate((pairs[:, 0], pairs[:, 1]), axis=2).reshape(
+            tokens // 2, 2 * rope_width
+        )
+
+    tail_body(
+        attention, total, rope_part, latent_ref, gain_ref, cos_ref, sin_ref, hidden_quad,
+        order_ref, rows_ref, out_ref, *refs,
+    )
+
+
+def fused(
+    key_up, value_up, hidden, latent_in, raw_key, gain, query, rope, cot, rows_out, dp_size
+):
+    tokens, rank = latent_in.shape
+    cols = hidden.shape[0]
+    rope_width = raw_key.shape[0]
+    heads = rope.shape[1] // rope_width
+    width = query.shape[1] // heads
+    scale_factor = 1.0 / math.sqrt(width + rope_width)
+    cos, sin = angle_tables(rope_width)
+    order, rows = tail_tables(rows_out)
     dma = pltpu.SemaphoreType.DMA
-    order, rows = tail_tables(rows_out)
+    full = (key_up.shape[0] * dp_size, key_up.shape[1])
+    any_spec = pl.BlockSpec(memory_space=pl.ANY)
     return pl.pallas_call(
-        tail_kernel,
-        out_shape=jax.ShapeDtypeStruct((rows_out, cols), F32),
-        in_specs=[VMEM_SPEC] * 9,
-        out_specs=VMEM_SPEC,
+        functools.partial(fused_kernel, scale_factor, width, heads // 2),
+        out_shape=(
+            jax.ShapeDtypeStruct(query.shape, BF16),
+            jax.ShapeDtypeStruct(rope.shape, BF16),
+            jax.ShapeDtypeStruct((rows_out, cols), F32),
+        ),
+        in_specs=[VMEM_SPEC] * 12 + [any_spec] * 3,
+        out_specs=(VMEM_SPEC,) * 3,
         scratch_shapes=[
-            pltpu.VMEM((HEAD_RANKS, CHUNK, latent_in.shape[1]), F32),
+            pltpu.VMEM(full, BF16),
+            pltpu.VMEM(full, BF16),
+            pltpu.VMEM((QUAD * cols, tokens), BF16),
+            pltpu.VMEM((tokens, rank), BF16),
+            pltpu.VMEM((tokens, rope_width), BF16),
+            pltpu.VMEM((tokens, rank), F32),
+            pltpu.VMEM((tokens, rope_width), F32),
+            pltpu.VMEM((tokens // 2, 2 * rope_width), F32),
+            pltpu.VMEM(query.shape, BF16),
+            pltpu.VMEM(rope.shape, BF16),
+            pltpu.VMEM(cot.shape, BF16),
+            dma((3,)),
+            dma((21,)), dma((21,)), dma((9,)), dma((9,)), dma((32,)), dma((32,)), dma((3,)),
+            dma((3,)), dma((3,)),
+            pltpu.VMEM((HEAD_RANKS, CHUNK, rank), F32),
             pltpu.VMEM((HEAD_RANKS, CHUNK // 2, 128), F32),
             pltpu.VMEM((CHUNK, LANES), BF16),
             pltpu.VMEM((QUAD, 2, CHUNK, 128), BF16),
@@ -592,8 +609,12 @@
             dma((HEAD_RANKS,)), dma((HEAD_RANKS,)),
         ],
         compiler_params=pltpu.CompilerParams(collective_id=1, has_side_effects=True),
-        name="tail",
-    )(part, rope_part, latent_in, gain, jnp.asarray(cos), jnp.asarray(sin), hidden_quad, jnp.asarray(order), jnp.asarray(rows))
+        name="fused",
+    )(
+        key_up, value_up, hidden, latent_in, raw_key, gain,
+        jnp.asarray(cos.T), jnp.asarray(sin.T), jnp.asarray(cos), jnp.asarray(sin),
+        jnp.asarray(order), jnp.asarray(rows), query, rope, cot,
+    )
 
 
 def local(
@@ -612,17 +633,10 @@
 ):
     row_count = latent_unnormed.shape[0]
     dp_size = lax.axis_size("dp")
-    cos, sin = angle_tables(unrotated_key.shape[1])
     gain = latent_norm_scale[None, :]
-    key_full, value_full, hidden_quad = gather_up(
-        key_up_matrix, value_up_matrix, hidden_in.T, dp_size
-    )
-    grad_query, grad_rope, part, rope_part = attention_back(
-        latent_unnormed, unrotated_key.T, gain, cos.T, sin.T,
-        plain_query_rows, rotated_query_rows, output_cotangent, key_full, value_full,
-    )
-    weight_sum = tail(
-        part, rope_part, latent_unnormed, gain, cos, sin, hidden_quad, down_weight.shape[0]
+    grad_query, grad_rope, weight_sum = fused(
+        key_up_matrix, value_up_matrix, hidden_in.T, latent_unnormed, unrotated_key.T, gain,
+        plain_query_rows, rotated_query_rows, output_cotangent, down_weight.shape[0], dp_size,
     )
     weight_grad = weight_sum / (row_count * dp_size)
     new_first = beta_one * first_moment + (1.0 - beta_one) * weight_grad

time: 94.3 us -> 88.7 us (0.941)
  Pallas kernels: 91.8 us -> 83.6 us
  local copies, waits for them, and re-layouts: 0.02 us -> 2.63 us
    pallas_call x3 -> x1, Pallas kernels: 91.8 us -> 83.6 us  [fused(): pl.pallas_call(functools.partial(fused_kernel, scale_factor, width, heads...]
    unnamed x6 -> x10, local copies, waits for them, and re-layouts: 0.02 us -> 2.63 us
where the time goes in v5:
time: 88.7 us; the launch traced here: 88.4 us
  Pallas kernels  83.6 us (94%)
  local copies, waits for them, and re-layouts  2.63 us (3%)
  other arithmetic  1.47 us (2%)
    pallas_call x1, Pallas kernels, fused(): pl.pallas_call(functools.partial(fused_kernel, scale_factor, width, heads...  83.6 us
    unnamed x10, local copies, waits for them, and re-layouts  2.63 us

profile of v5, /device:TPU:1, one launch (start us, length us, event | category | flops | bytes accessed | tf_op | source)
XLA Modules:
  0.0 88.4 jit_solution(5749315060286560747)
XLA Ops:
  0.6 0.0 copy-start.1
  0.6 0.0 copy-start.2
  0.7 0.0 copy-start.3
  0.7 83.6 %fused.1 = (bf16[256,1024]{1,0:T(8,128)(2,1)}, bf16[256,512]{1,0:T(8,128)(2,1)}, f32[18,448]{1,0:T(8,128)}) custom-call(bf16[16,1024]{1,0:T(8,128)(2,1)} %refs_0_.1, bf16[16,1024]{1,0:T(8,128)(2,1)} %refs_1_.1, bf16[448,256]{1,0:T(8,128)(2,1)} %bitcast.3, bf16[256,512]{1,0:T(8,128)(2,1)} %refs_3_.1, bf16[64,256]{1,0:T(8,128)(2,1)} %bitcast.4, ...), custom_call_target="tpu_custom_call" | custom-call | tf_op jit(solution)/shard_map/fused/pallas_call | solution.py:574
  84.3 0.0 copy-done.1
  84.3 0.0 copy-done.2
  84.3 0.0 copy-done.3
  84.3 1.5 %multiply_subtract_fusion = (f32[18,448]{1,0:T(8,128)}, f32[18,448]{1,0:T(8,128)}, f32[18,448]{1,0:T(8,128)}) fusion(f32[18,448]{1,0:T(8,128)S(1)} %copy-done.1, f32[18,448]{1,0:T(8,128)} %get-tuple-element.10, f32[18,448]{1,0:T(8,128)S(1)} %copy-done.2, f32[18,448]{1,0:T(8,128)S(1)} %copy-done.3), kind=kLoop, calls=%fused_computation | loop fusion | flops 129024 | bytes 225792 | tf_op jit(solution)/shard_map/sub | solution.py:645
  85.8 0.0 copy-start
  85.8 1.9 %copy.25 = bf16[256,1024]{1,0:T(8,128)(2,1)} copy(bf16[256,1024]{1,0:T(8,128)(2,1)} %get-tuple-element.19) | data formatting | bytes 1048576
  87.7 0.0 copy-done
  87.7 0.7 copy.26
Async XLA Ops:
  0.6 83.7 %copy-start.1 = (f32[18,448]{1,0:T(8,128)S(1)}, f32[18,448]{1,0:T(8,128)}, u32[]{:S(2)}) copy-start(f32[18,448]{1,0:T(8,128)} %param.27) | copy-start | bytes 96772
  0.6 83.7 %copy-start.2 = (f32[18,448]{1,0:T(8,128)S(1)}, f32[18,448]{1,0:T(8,128)}, u32[]{:S(2)}) copy-start(f32[18,448]{1,0:T(8,128)} %param.28) | copy-start | bytes 96772
  0.7 83.7 %copy-start.3 = (f32[18,448]{1,0:T(8,128)S(1)}, f32[18,448]{1,0:T(8,128)}, u32[]{:S(2)}) copy-start(f32[18,448]{1,0:T(8,128)} %param.29) | copy-start | bytes 96772
  85.8 1.9 %copy-start = (bf16[256,512]{1,0:T(8,128)(2,1)S(1)}, bf16[256,512]{1,0:T(8,128)(2,1)}, u32[]{:S(2)}) copy-start(bf16[256,512]{1,0:T(8,128)(2,1)} %get-tuple-element.20) | copy-start | bytes 786436

commit v6 on v5

--- a/solution.py
+++ b/solution.py
@@ -220,7 +220,7 @@
     rope_width = key_rot.shape[1]
 
     def columns(size):
-        return pl.ds(pl.multiple_of(pair * size, size), size)
+        return slice(pair * size, (pair + 1) * size)
 
     both = columns(2 * width)
     key_up, value_up = key_up_ref[:, both], value_up_ref[:, both]
@@ -537,8 +537,7 @@
         for copy in copies:
             copy.wait()
 
-        @pl.loop(0, count)
-        def _(pair):
+        for pair in range(count):
             attention_pair(
                 scale_factor, width, pair, *buffers, key_full, value_full,
                 grad_query_ref, grad_rope_ref, latent, key_rot, total, rope_total,
@@ -617,6 +616,58 @@
     )
 
 
+def finish_kernel(
+    token_total, query_in, rope_in, sum_ref, weight_ref, first_ref, second_ref,
+    query_out, rope_out, new_weight_ref, new_first_ref, new_second_ref,
+    query_buffer, rope_buffer, sems,
+):
+    chain = ((query_in, query_buffer, query_out), (rope_in, rope_buffer, rope_out))
+    loads = [
+        pltpu.make_async_copy(source, buffer, sems.at[n])
+        for n, (source, buffer, _) in enumerate(chain)
+    ]
+    stores = [
+        pltpu.make_async_copy(buffer, target, sems.at[2 + n])
+        for n, (_, buffer, target) in enumerate(chain)
+    ]
+    for copy in loads:
+        copy.start()
+    for n in range(2):
+        loads[n].wait()
+        stores[n].start()
+    weight_grad = sum_ref[...] / token_total
+    new_first = beta_one * first_ref[...] + (1.0 - beta_one) * weight_grad
+    new_second = beta_two * second_ref[...] + (1.0 - beta_two) * weight_grad * weight_grad
+    direction = new_first / bias_one / (jnp.sqrt(new_second / bias_two) + adam_eps)
+    weight = weight_ref[...]
+    new_weight_ref[...] = weight - learn_rate * (direction + decay_rate * weight)
+    new_first_ref[...] = new_first
+    new_second_ref[...] = new_second
+    for copy in stores:
+        copy.wait()
+
+
+def finish_step(token_total, grad_query, grad_rope, weight_sum, weight, first, second):
+    any_spec = pl.BlockSpec(memory_space=pl.ANY)
+    small = jax.ShapeDtypeStruct(weight.shape, F32)
+    return pl.pallas_call(
+        functools.partial(finish_kernel, float(token_total)),
+        out_shape=(
+            jax.ShapeDtypeStruct(grad_query.shape, BF16),
+            jax.ShapeDtypeStruct(grad_rope.shape, BF16),
+            small, small, small,
+        ),
+        in_specs=[any_spec] * 2 + [VMEM_SPEC] * 4,
+        out_specs=(any_spec, any_spec, VMEM_SPEC, VMEM_SPEC, VMEM_SPEC),
+        scratch_shapes=[
+            pltpu.VMEM(grad_query.shape, BF16),
+            pltpu.VMEM(grad_rope.shape, BF16),
+            pltpu.SemaphoreType.DMA((4,)),
+        ],
+        name="finish_step",
+    )(grad_query, grad_rope, weight_sum, weight, first, second)
+
+
 def local(
     hidden_in,
     latent_unnormed,
@@ -638,12 +689,10 @@
         key_up_matrix, value_up_matrix, hidden_in.T, latent_unnormed, unrotated_key.T, gain,
         plain_query_rows, rotated_query_rows, output_cotangent, down_weight.shape[0], dp_size,
     )
-    weight_grad = weight_sum / (row_count * dp_size)
-    new_first = beta_one * first_moment + (1.0 - beta_one) * weight_grad
-    new_second = beta_two * second_moment + (1.0 - beta_two) * weight_grad * weight_grad
-    direction = new_first / bias_one / (jnp.sqrt(new_second / bias_two) + adam_eps)
-    new_weight = down_weight - learn_rate * (direction + decay_rate * down_weight)
-    return grad_query, grad_rope, new_weight, new_first, new_second
+    return finish_step(
+        row_count * dp_size, grad_query, grad_rope, weight_sum,
+        down_weight, first_moment, second_moment,
+    )
 
 
 def solution(mesh):

time: 88.7 us -> 87.2 us (0.983)
  Pallas kernels: 83.6 us -> 86.3 us
  local copies, waits for them, and re-layouts: 2.63 us -> 0 us
  other arithmetic: 1.47 us -> 0 us
    pallas_call x0 -> x1, Pallas kernels: none -> 3.48 us  [finish_step(): pl.pallas_call(functools.partial(finish_kernel, float(token_total)), out_...]
    unnamed x10 -> x0, local copies, waits for them, and re-layouts: 2.63 us -> none
    sub x1 -> x0, other arithmetic: 1.47 us -> none  [local(): down_weight - learn_rate * (direction + decay_rate * down_weight)]
where the time goes in v6:
time: 87.2 us; the launch traced here: 87 us
  Pallas kernels  86.3 us (99%)
    pallas_call x1, Pallas kernels, fused(): pl.pallas_call(functools.partial(fused_kernel, scale_factor, width, heads...  82.9 us
    pallas_call x1, Pallas kernels, finish_step(): pl.pallas_call(functools.partial(finish_kernel, float(token_total)), out_...  3.48 us

profile of v6, /device:TPU:1, one launch (start us, length us, event | category | flops | bytes accessed | tf_op | source)
XLA Modules:
  0.0 87.0 jit_solution(1998072832071198016)
XLA Ops:
  0.6 82.9 %fused.1 = (bf16[256,1024]{1,0:T(8,128)(2,1)}, bf16[256,512]{1,0:T(8,128)(2,1)}, f32[18,448]{1,0:T(8,128)}) custom-call(bf16[16,1024]{1,0:T(8,128)(2,1)} %refs_0_.1, bf16[16,1024]{1,0:T(8,128)(2,1)} %refs_1_.1, bf16[448,256]{1,0:T(8,128)(2,1)} %bitcast.3, bf16[256,512]{1,0:T(8,128)(2,1)} %refs_3_.1, bf16[64,256]{1,0:T(8,128)(2,1)} %bitcast.4, ...), custom_call_target="tpu_custom_call" | custom-call | tf_op jit(solution)/shard_map/fused/pallas_call | solution.py:573
  83.5 3.5 %finish_step.1 = (bf16[256,1024]{1,0:T(8,128)(2,1)}, bf16[256,512]{1,0:T(8,128)(2,1)}, f32[18,448]{1,0:T(8,128)}, f32[18,448]{1,0:T(8,128)}, f32[18,448]{1,0:T(8,128)}) custom-call(bf16[256,1024]{1,0:T(8,128)(2,1)} %get-tuple-element.8.query_in, bf16[256,512]{1,0:T(8,128)(2,1)} %get-tuple-element.9.rope_in, f32[18,448]{1,0:T(8,128)} %get-tuple-element.10.sum_ref, ...), custom_call_target="tpu_custom_call" | custom-call | tf_op jit(solution)/shard_map/finish_step/pallas_call | solution.py:653

commit v7 on v6

--- a/solution.py
+++ b/solution.py
@@ -513,15 +513,21 @@
     key_in, value_in, hidden_in, latent_ref, raw_ref, gain_ref = take(6)
     cos_t, sin_t, cos_ref, sin_ref, order_ref, rows_ref = take(6)
     loads = take(3)
-    grad_query_ref, grad_rope_ref, out_ref = take(3)
+    query_out, rope_out, out_ref = take(3)
     key_full, value_full, hidden_quad = take(3)
     latent, key_rot, total, rope_total, rope_part = take(5)
     buffers = take(3)
+    grad_query_ref, grad_rope_ref = take(2)
     load_sem = take(1)[0]
     gather_sems = take(9)
 
     copies = [
         pltpu.make_async_copy(loads[n], buffers[n], load_sem.at[n]) for n in range(3)
+    ]
+
+    stores = [
+        pltpu.make_async_copy(grad_query_ref, query_out, load_sem.at[3]),
+        pltpu.make_async_copy(grad_rope_ref, rope_out, load_sem.at[4]),
     ]
 
     def attention(enter):
@@ -543,6 +549,8 @@
                 grad_query_ref, grad_rope_ref, latent, key_rot, total, rope_total,
             )
 
+        for copy in stores:
+            copy.start()
         finish()
         tokens, rope_width = rope_total.shape
         pairs = rope_total[...].reshape(tokens // CHUNK, 2, CHUNK // 2, rope_width)
@@ -554,6 +562,8 @@
         attention, total, rope_part, latent_ref, gain_ref, cos_ref, sin_ref, hidden_quad,
         order_ref, rows_ref, out_ref, *refs,
     )
+    for copy in stores:
+        copy.wait()
 
 
 def fused(
@@ -578,7 +588,7 @@
             jax.ShapeDtypeStruct((rows_out, cols), F32),
         ),
         in_specs=[VMEM_SPEC] * 12 + [any_spec] * 3,
-        out_specs=(VMEM_SPEC,) * 3,
+        out_specs=(any_spec, any_spec, VMEM_SPEC),
         scratch_shapes=[
             pltpu.VMEM(full, BF16),
             pltpu.VMEM(full, BF16),
@@ -591,7 +601,9 @@
             pltpu.VMEM(query.shape, BF16),
             pltpu.VMEM(rope.shape, BF16),
             pltpu.VMEM(cot.shape, BF16),
-            dma((3,)),
+            pltpu.VMEM(query.shape, BF16),
+            pltpu.VMEM(rope.shape, BF16),
+            dma((5,)),
             dma((21,)), dma((21,)), dma((9,)), dma((9,)), dma((32,)), dma((32,)), dma((3,)),
             dma((3,)), dma((3,)),
             pltpu.VMEM((HEAD_RANKS, CHUNK, rank), F32),

time: 87.2 us -> 87.2 us (level)
  no operation moved by 1% of the time
where the time goes in v7:
time: 87.2 us; the launch traced here: 87 us
  Pallas kernels  86.3 us (99%)
    pallas_call x1, Pallas kernels, fused(): pl.pallas_call(functools.partial(fused_kernel, scale_factor, width, heads...  82.8 us
    pallas_call x1, Pallas kernels, finish_step(): pl.pallas_call(functools.partial(finish_kernel, float(token_total)), out_...  3.48 us

profile of v7, /device:TPU:1, one launch (start us, length us, event | category | flops | bytes accessed | tf_op | source)
XLA Modules:
  0.0 87.0 jit_solution(11998171171174517676)
XLA Ops:
  0.6 82.8 %fused.1 = (bf16[256,1024]{1,0:T(8,128)(2,1)}, bf16[256,512]{1,0:T(8,128)(2,1)}, f32[18,448]{1,0:T(8,128)}) custom-call(bf16[16,1024]{1,0:T(8,128)(2,1)} %refs_0_.1, bf16[16,1024]{1,0:T(8,128)(2,1)} %refs_1_.1, bf16[448,256]{1,0:T(8,128)(2,1)} %bitcast.3, bf16[256,512]{1,0:T(8,128)(2,1)} %refs_3_.1, bf16[64,256]{1,0:T(8,128)(2,1)} %bitcast.4, ...), custom_call_target="tpu_custom_call" | custom-call | tf_op jit(solution)/shard_map/fused/pallas_call | solution.py:583
  83.5 3.5 %finish_step.1 = (bf16[256,1024]{1,0:T(8,128)(2,1)}, bf16[256,512]{1,0:T(8,128)(2,1)}, f32[18,448]{1,0:T(8,128)}, f32[18,448]{1,0:T(8,128)}, f32[18,448]{1,0:T(8,128)}) custom-call(bf16[256,1024]{1,0:T(8,128)(2,1)} %get-tuple-element.8.query_in, bf16[256,512]{1,0:T(8,128)(2,1)} %get-tuple-element.9.rope_in, f32[18,448]{1,0:T(8,128)} %get-tuple-element.10.sum_ref, ...), custom_call_target="tpu_custom_call" | custom-call | tf_op jit(solution)/shard_map/finish_step/pallas_call | solution.py:665
